TPU v7x, 512 devices: a whole 4x4x16 slice. The times are simulated.
512 devices in a mesh: ctx: 64 (over z_lo, x, core), head: 8 (over z_hi, y).
Axes of the slice: x: 4, y: 4, z: 16 (z_hi: 2, z_lo: 8; z = z_hi * 8 + z_lo), core: 2. Of those that a mesh axis runs over, the one named last changes fastest.
Arguments:
- context_queries: bfloat16 [16384, 8192], P('ctx', 'head'), may hold values from -7 to 7
- context_keys: bfloat16 [16384, 1024], P('ctx', 'head'), may hold values from -7 to 7
- context_values: bfloat16 [16384, 1024], P('ctx', 'head'), may hold values from -6 to 6
- option_query_rows: bfloat16 [128, 8192], P(None, 'head'), may hold values from -7 to 7
- option_key_rows: bfloat16 [128, 1024], P(None, 'head'), may hold values from -3 to 3
- option_value_rows: bfloat16 [128, 1024], P(None, 'head'), may hold values from -6 to 6
- option_segments: int32 [128], replicated, may hold values from 0 to 7, never falling along the last dimension, each value on 1 to 32 neighbouring positions
- out_weight: bfloat16 [8192, 8192], P('head', 'ctx'), may hold values from -0.75 to 0.75
Outputs:
- context_output: bfloat16 [16384, 8192], P('ctx', 'head')
- option_out: bfloat16 [128, 8192], P('head', 'ctx')
All inputs are finite; a program needn't handle non-finite values.
Results may differ from a plain program's by a relative error of at most 0.014.
Values may be sent and summed in bfloat16 or wider, within the bound.
A program may use at most 64 MiB of HBM per device.

v0:
```python
import math

import jax
import jax.numpy as jnp
from jax import lax
from jax.sharding import PartitionSpec as P

HEAD_SIZE = 128
OPTION_ROWS = 128


far_below = -1e30


def from_root(x, axis, root):
    return lax.dynamic_index_in_dim(lax.all_gather(x, axis), root, 0, keepdims=False)


def from_everyone(x, axis):
    count = lax.axis_size(axis)
    return lax.all_to_all(jnp.broadcast_to(x[None], (count, *x.shape)), axis, 0, 0, tiled=True)


def over_copies(x, axis):
    everything = from_everyone(x, axis)
    return jnp.max(everything, axis=0)


def in_blocks(x, dim, count):
    before, after = (x.shape[:dim], x.shape[dim + 1 :])
    return jnp.moveaxis(x.reshape(*before, count, -1, *after), dim, 0)


def sum_at_owner(x, axis, dim):
    parts = in_blocks(x, dim, lax.axis_size(axis))
    arrived = lax.all_to_all(parts, axis, split_axis=0, concat_axis=0, tiled=True)
    return arrived.sum(axis=0)


def in_one_piece(arrays, axis, dim, along):
    widths = [math.prod(a.shape[along:]) for a in arrays]
    both = jnp.concatenate(
        [a.reshape(*a.shape[:along], w) for a, w in zip(arrays, widths)], axis=along
    )
    result = sum_at_owner(both, axis, dim)
    parts = jnp.split(result, [sum(widths[:k]) for k in range(1, len(widths))], axis=along)
    return tuple(
        (b.reshape(*result.shape[:along], *a.shape[along:]) for a, b in zip(arrays, parts))
    )


def in_order(parts, dim):
    parts = jnp.moveaxis(parts, 0, dim)
    shape = parts.shape
    return parts.reshape(*shape[:dim], shape[dim] * shape[dim + 1], *shape[dim + 2 :])


def collect(x, axis, dim):
    parts = from_everyone(x, axis)
    return in_order(parts, dim)


def sent_and_summed(x, axis, dim):
    parts = in_blocks(x, dim, lax.axis_size(axis))
    arrived = lax.all_to_all(parts, axis, split_axis=0, concat_axis=0, tiled=True)
    return arrived.astype(jnp.float32).sum(axis=0)


def combine_parts(first_part, second_part):
    top_first, sum_first, mix_first = first_part
    top_second, sum_second, mix_second = second_part
    joined_top = jnp.maximum(top_first, top_second)
    factor_first = jnp.exp(top_first - joined_top)
    factor_second = jnp.exp(top_second - joined_top)
    joined_sum = sum_first * factor_first + sum_second * factor_second
    joined_mix = mix_first * factor_first[..., None] + mix_second * factor_second[..., None]
    return (joined_top, joined_sum, joined_mix)


def shards(
    context_queries,
    context_keys,
    context_values,
    option_query_rows,
    option_key_rows,
    option_value_rows,
    option_segments,
    out_weight,
):
    block_len = context_queries.shape[0]
    kv_local = context_keys.shape[1] // HEAD_SIZE
    head_groups = context_queries.shape[1] // (kv_local * HEAD_SIZE)
    score_scale = HEAD_SIZE ** (-0.5)
    block_index = lax.axis_index("ctx")
    stacked = jnp.stack([context_keys, context_values])
    anchor = from_root(stacked, "ctx", 0)
    block_own_keys = context_keys.reshape(block_len, kv_local, HEAD_SIZE)
    block_own_values = context_values.reshape(block_len, kv_local, HEAD_SIZE)
    keys_anchor = anchor[0].reshape(block_len, kv_local, HEAD_SIZE)
    values_anchor = anchor[1].reshape(block_len, kv_local, HEAD_SIZE)
    query_head_count = context_queries.reshape(block_len, kv_local, head_groups, HEAD_SIZE)
    positions = jnp.arange(block_len)
    causal = (positions[:, None] >= positions[None, :])[:, None, None, :]
    own_scores = (
        jnp.einsum(
            "tkgd,skd->tkgs", query_head_count, block_own_keys, preferred_element_type=jnp.float32
        )
        * score_scale
    )
    own_scores = jnp.where(causal, own_scores, far_below)
    anchor_scores = (
        jnp.einsum(
            "tkgd,skd->tkgs", query_head_count, keys_anchor, preferred_element_type=jnp.float32
        )
        * score_scale
    )
    anchor_scores = jnp.where(block_index > 0, anchor_scores, far_below)
    row_top = jnp.maximum(jnp.max(own_scores, axis=-1), jnp.max(anchor_scores, axis=-1))
    own_probs = jnp.exp(own_scores - row_top[..., None])
    anchor_probs = jnp.exp(anchor_scores - row_top[..., None])
    row_sum = jnp.sum(own_probs, axis=-1) + jnp.sum(anchor_probs, axis=-1)
    row_mix = jnp.einsum(
        "tkgs,skd->tkgd",
        own_probs.astype(jnp.bfloat16),
        block_own_values,
        preferred_element_type=jnp.float32,
    )
    row_mix = row_mix + jnp.einsum(
        "tkgs,skd->tkgd",
        anchor_probs.astype(jnp.bfloat16),
        values_anchor,
        preferred_element_type=jnp.float32,
    )
    context_output = (
        (row_mix / row_sum[..., None])
        .astype(jnp.bfloat16)
        .reshape(block_len, kv_local * head_groups * HEAD_SIZE)
    )
    option_heads = option_query_rows.reshape(OPTION_ROWS, kv_local, head_groups, HEAD_SIZE)
    ctx_opt_scores = (
        jnp.einsum(
            "rkgd,skd->rkgs", option_heads, block_own_keys, preferred_element_type=jnp.float32
        )
        * score_scale
    )
    local_top = jnp.max(ctx_opt_scores, axis=-1)
    local_probs = jnp.exp(ctx_opt_scores - local_top[..., None])
    local_sum = jnp.sum(local_probs, axis=-1)
    local_mix = jnp.einsum(
        "rkgs,skd->rkgd",
        local_probs.astype(jnp.bfloat16),
        block_own_values,
        preferred_element_type=jnp.float32,
    )
    self_keys = option_key_rows.reshape(OPTION_ROWS, kv_local, HEAD_SIZE)
    self_values = option_value_rows.reshape(OPTION_ROWS, kv_local, HEAD_SIZE)
    option_rows = jnp.arange(OPTION_ROWS)
    global_top = over_copies(local_top, "ctx")
    factor = jnp.exp(local_top - global_top)
    share_mix, share_sum = in_one_piece(
        (local_mix * factor[..., None], local_sum * factor), "ctx", 0, 3
    )
    row_count = OPTION_ROWS // lax.axis_size("ctx")
    first_row = block_index * row_count
    top_rows = lax.dynamic_slice_in_dim(global_top, first_row, row_count, 0)
    queries_here = lax.dynamic_slice_in_dim(option_heads, first_row, row_count, 0)
    segment_here = lax.dynamic_slice_in_dim(option_segments, first_row, row_count, 0)
    rows_here = first_row + jnp.arange(row_count)
    visible = (segment_here[:, None] == option_segments[None, :]) & (
        rows_here[:, None] >= option_rows[None, :]
    )
    self_scores = (
        jnp.einsum("rkgd,skd->rkgs", queries_here, self_keys, preferred_element_type=jnp.float32)
        * score_scale
    )
    self_scores = jnp.where(visible[:, None, None, :], self_scores, far_below)
    self_top = jnp.max(self_scores, axis=-1)
    self_probs = jnp.exp(self_scores - self_top[..., None])
    self_sum = jnp.sum(self_probs, axis=-1)
    self_mix = jnp.einsum(
        "rkgs,skd->rkgd",
        self_probs.astype(jnp.bfloat16),
        self_values,
        preferred_element_type=jnp.float32,
    )
    joined_top, joined_sum, joined_mix = combine_parts(
        (top_rows, share_sum, share_mix), (self_top, self_sum, self_mix)
    )
    piece_rows = (
        (joined_mix / joined_sum[..., None])
        .astype(jnp.bfloat16)
        .reshape(row_count, kv_local * head_groups * HEAD_SIZE)
    )
    attended = collect(piece_rows, "ctx", 0)
    rows_here = attended
    option_out = sent_and_summed(
        jnp.dot(rows_here, out_weight, preferred_element_type=jnp.float32).astype(jnp.bfloat16),
        "head",
        0,
    ).astype(jnp.bfloat16)
    return (context_output, option_out)


def solution(mesh):
    placed = (
        P("ctx", "head"),
        P("ctx", "head"),
        P("ctx", "head"),
        P(None, "head"),
        P(None, "head"),
        P(None, "head"),
        P(),
        P("head", "ctx"),
    )
    return jax.shard_map(
        shards,
        mesh=mesh,
        in_specs=placed,
        out_specs=(P("ctx", "head"), P("head", "ctx")),
        check_vma=False,
    )
```

profile of v0, /device:TPU:1, one launch (start us, length us, event | category | flops | bytes accessed | tf_op | source)
XLA Modules:
  0.0 196.9 jit_solution(13297053719456197422)
XLA Ops:
  7.2 1.6 pad_maximum_fusion.1
  8.8 1.3 fusion.66
  10.2 0.7 broadcast_in_dim.37
  10.9 17.0 %all-to-all-start = ((f32[64,128,1,8]{1,3,2,0:T(8,128)}), f32[64,128,1,8]{1,3,2,0:T(8,128)S(1)}, u32[]{:S(2)}, u32[]{:S(2)}) async-start(f32[64,128,1,8]{1,3,2,0:T(8,128)} %broadcast_in_dim.37), calls=%async_computation | async-start | bytes 524288 | tf_op jit(solution)/shard_map/all_to_all | solution.py:21
  28.1 21.8 %all-to-all-done = f32[64,128,1,8]{1,3,2,0:T(8,128)S(1)} async-done(((f32[64,128,1,8]{1,3,2,0:T(8,128)}), f32[64,128,1,8]{1,3,2,0:T(8,128)S(1)}, u32[]{:S(2)}, u32[]{:S(2)}) %all-to-all-start) | async-done | bytes 262176 | tf_op jit(solution)/shard_map/all_to_all | solution.py:21
  50.0 0.8 copy.81
  51.3 1.6 pad_maximum_fusion
  52.9 5.6 %all-to-all-start.1 = ((f32[64,2,1,8,129]{4,1,3,2,0:T(2,128)}), f32[64,2,1,8,129]{4,1,3,2,0:T(2,128)S(1)}, u32[]{:S(2)}, u32[]{:S(2)}) async-start(f32[64,2,1,8,129]{4,1,3,2,0:T(2,128)} %pad_maximum_fusion), calls=%async_computation.1 | async-start | bytes 2097152 | tf_op jit(solution)/shard_map/all_to_all | solution.py:36
  59.3 60.5 %all-to-all-done.1 = f32[64,2,1,8,129]{4,1,3,2,0:T(2,128)S(1)} async-done(((f32[64,2,1,8,129]{4,1,3,2,0:T(2,128)}), f32[64,2,1,8,129]{4,1,3,2,0:T(2,128)S(1)}, u32[]{:S(2)}, u32[]{:S(2)}) %all-to-all-start.1) | async-done | bytes 528416 | tf_op jit(solution)/shard_map/all_to_all | solution.py:36
  119.8 0.4 reduce_sum.62
  120.9 0.8 broadcast_in_dim.41
  121.7 6.6 %all-to-all-start.2 = ((bf16[64,2,1024]{2,1,0:T(2,128)(2,1)}), bf16[64,2,1024]{2,1,0:T(2,128)(2,1)S(1)}, u32[]{:S(2)}, u32[]{:S(2)}) async-start(bf16[64,2,1024]{2,1,0:T(2,128)(2,1)} %broadcast_in_dim.41), calls=%async_computation.2 | async-start | bytes 524288 | tf_op jit(solution)/shard_map/all_to_all | solution.py:21
  128.4 22.5 %all-to-all-done.2 = bf16[64,2,1024]{2,1,0:T(2,128)(2,1)S(1)} async-done(((bf16[64,2,1024]{2,1,0:T(2,128)(2,1)}), bf16[64,2,1024]{2,1,0:T(2,128)(2,1)S(1)}, u32[]{:S(2)}, u32[]{:S(2)}) %all-to-all-start.2) | async-done | bytes 262176 | tf_op jit(solution)/shard_map/all_to_all | solution.py:21
  151.0 0.8 convolution_convert_fusion
  151.8 9.0 %all-to-all-start.3 = ((bf16[8,16,128]{2,1,0:T(8,128)(2,1)}), bf16[8,16,128]{2,1,0:T(8,128)(2,1)S(1)}, u32[]{:S(2)}, u32[]{:S(2)}) async-start(bf16[8,16,128]{2,1,0:T(8,128)(2,1)} %bitcast.42), calls=%async_computation.3 | async-start | bytes 65536 | tf_op jit(solution)/shard_map/all_to_all | solution.py:65
  160.9 0.5 fusion.65
  161.4 13.4 %all-to-all-done.3 = bf16[8,16,128]{2,1,0:T(8,128)(2,1)S(1)} async-done(((bf16[8,16,128]{2,1,0:T(8,128)(2,1)}), bf16[8,16,128]{2,1,0:T(8,128)(2,1)S(1)}, u32[]{:S(2)}, u32[]{:S(2)}) %all-to-all-start.3) | async-done | bytes 32800 | tf_op jit(solution)/shard_map/all_to_all | solution.py:65
  174.8 0.6 reduce_sum.65
  175.4 9.6 %all-gather.3.cloned.1.call-done = bf16[128,256,128]{2,1,0:T(8,128)(2,1)} async-done(((bf16[2,256,128]{2,1,0:T(8,128)(2,1)}), bf16[128,256,128]{2,1,0:T(8,128)(2,1)}) %all-gather.3.cloned.1.call-update) | async-done | bytes 8388624 | tf_op jit(solution)/shard_map/all_gather | solution.py:16
  185.0 1.3 bitcast_reduce_fusion
  186.3 0.5 convolution_bitcast_fusion
  186.8 0.7 fusion.3
  187.6 1.5 fusion.21
  189.0 1.0 copy.91
  (44 shorter events, 2.4 us)
Async XLA Ops:
  7.2 153.7 %copy-start = (bf16[256,1024]{1,0:T(8,128)(2,1)S(1)}, bf16[256,1024]{1,0:T(8,128)(2,1)}, u32[]{:S(2)}) copy-start(bf16[256,1024]{1,0:T(8,128)(2,1)} %param.8) | copy-start | bytes 1572868
  7.2 177.8 %all-gather.3.cloned.1.call-start = ((), (), s32[]{:S(2)}) async-start(), calls=%async_computation.4 | async-start | bytes 8519680 | tf_op jit(solution)/shard_map/all_gather | solution.py:16
  8.8 42.0 %copy-start.2 = (bf16[256,128]{1,0:T(8,128)(2,1)S(1)}, bf16[256,128]{1,0:T(8,128)(2,1)}, u32[]{:S(2)}) copy-start(bf16[256,128]{1,0:T(8,128)(2,1)} %param.10) | copy-start | bytes 196612
  10.9 39.0 %all-to-all-start = ((f32[64,128,1,8]{1,3,2,0:T(8,128)}), f32[64,128,1,8]{1,3,2,0:T(8,128)S(1)}, u32[]{:S(2)}, u32[]{:S(2)}) async-start(f32[64,128,1,8]{1,3,2,0:T(8,128)} %broadcast_in_dim.37), calls=%async_computation | async-start | bytes 524288 | tf_op jit(solution)/shard_map/all_to_all | solution.py:21
  51.2 7.3 %copy-start.1 = (bf16[128,1024]{1,0:T(8,128)(2,1)S(1)}, bf16[128,1024]{1,0:T(8,128)(2,1)}, u32[]{:S(2)}) copy-start(bf16[128,1024]{1,0:T(8,128)(2,1)} %param.11) | copy-start | bytes 786436
  51.3 7.3 %copy-start.6 = (s32[128]{0:T(128)S(1)}, s32[128]{0:T(128)}, u32[]{:S(2)}) copy-start(s32[128]{0:T(128)} %param.14) | copy-start | bytes 1540
  51.3 7.5 %copy-start.5 = (bf16[128,128]{1,0:T(8,128)(2,1)S(1)}, bf16[128,128]{1,0:T(8,128)(2,1)}, u32[]{:S(2)}) copy-start(bf16[128,128]{1,0:T(8,128)(2,1)} %param.12) | copy-start | bytes 98308
  52.9 67.8 %copy-start.7 = (bf16[128,128]{1,0:T(8,128)(2,1)S(1)}, bf16[128,128]{1,0:T(8,128)(2,1)}, u32[]{:S(2)}) copy-start(bf16[128,128]{1,0:T(8,128)(2,1)} %param.13) | copy-start | bytes 98308
  52.9 66.9 %all-to-all-start.1 = ((f32[64,2,1,8,129]{4,1,3,2,0:T(2,128)}), f32[64,2,1,8,129]{4,1,3,2,0:T(2,128)S(1)}, u32[]{:S(2)}, u32[]{:S(2)}) async-start(f32[64,2,1,8,129]{4,1,3,2,0:T(2,128)} %pad_maximum_fusion), calls=%async_computation.1 | async-start | bytes 2097152 | tf_op jit(solution)/shard_map/all_to_all | solution.py:36
  58.5 92.5 %copy-start.4 = (bf16[1024,128]{1,0:T(8,128)(2,1)S(1)}, bf16[1024,128]{1,0:T(8,128)(2,1)}, u32[]{:S(2)}) copy-start(bf16[1024,128]{1,0:T(8,128)(2,1)} %param.15) | copy-start | bytes 786436
  58.5 102.4 %copy-start.3 = (bf16[256,128]{1,0:T(8,128)(2,1)S(1)}, bf16[256,128]{1,0:T(8,128)(2,1)}, u32[]{:S(2)}) copy-start(bf16[256,128]{1,0:T(8,128)(2,1)} %param.9) | copy-start | bytes 196612
  121.7 29.2 %all-to-all-start.2 = ((bf16[64,2,1024]{2,1,0:T(2,128)(2,1)}), bf16[64,2,1024]{2,1,0:T(2,128)(2,1)S(1)}, u32[]{:S(2)}, u32[]{:S(2)}) async-start(bf16[64,2,1024]{2,1,0:T(2,128)(2,1)} %broadcast_in_dim.41), calls=%async_computation.2 | async-start | bytes 524288 | tf_op jit(solution)/shard_map/all_to_all | solution.py:21
  151.8 23.0 %all-to-all-start.3 = ((bf16[8,16,128]{2,1,0:T(8,128)(2,1)}), bf16[8,16,128]{2,1,0:T(8,128)(2,1)S(1)}, u32[]{:S(2)}, u32[]{:S(2)}) async-start(bf16[8,16,128]{2,1,0:T(8,128)(2,1)} %bitcast.42), calls=%async_computation.3 | async-start | bytes 65536 | tf_op jit(solution)/shard_map/all_to_all | solution.py:65
Sparse Core Ops, SparseCore 0:
  10.1 174.8 all-gather.2
where the time goes:
time: 197 us
  waiting for transfers between devices  128 us (65%)
  starting transfers between devices  38.3 us (19%)
  between operations  14.3 us (7%)
  matrix products  6.67 us (3%)
  other arithmetic  5.55 us (3%)
  local copies, waits for them, and re-layouts  4.33 us (2%)
    all_to_all x1, waiting for transfers between devices, sum_at_owner(): lax.all_to_all(parts, axis, split_axis=0, concat_axis=0, tiled=True)  60.5 us
    all_to_all x2, waiting for transfers between devices, from_everyone(): lax.all_to_all(jnp.broadcast_to(x[None], (count, *x.shape)), axis, 0, 0,...  44.3 us
    all_to_all x2, starting transfers between devices, from_everyone(): lax.all_to_all(jnp.broadcast_to(x[None], (count, *x.shape)), axis, 0, 0,...  23.6 us
    all_to_all x1, waiting for transfers between devices, sent_and_summed(): lax.all_to_all(parts, axis, split_axis=0, concat_axis=0, tiled=True)  13.4 us
    all_gather x1, waiting for transfers between devices, from_root(): lax.all_gather(x, axis)  9.58 us
    all_to_all x1, starting transfers between devices, sent_and_summed(): lax.all_to_all(parts, axis, split_axis=0, concat_axis=0, tiled=True)  9.04 us
    all_to_all x1, starting transfers between devices, sum_at_owner(): lax.all_to_all(parts, axis, split_axis=0, concat_axis=0, tiled=True)  5.58 us
  transfers between devices with their start and end apart: 5, of which 5 were waited for; matrix products, arithmetic and copies ran while one was open for 5% of the time, Pallas kernels for 0%

commit v1 on v0

v1 whole, which is shorter than its diff:
```python
import functools

import jax
import jax.numpy as jnp
from jax import lax
from jax.experimental import pallas as pl
from jax.experimental.pallas import tpu as pltpu
from jax.sharding import PartitionSpec as P

MESH = pl.DeviceIdType.MESH
HEAD = 128
ROWS = 128
BLOCK = 256
GROUPS = 8
NZ = 8
SCALE = HEAD ** (-0.5)
FAR = -1e30
F32 = jnp.float32
BF16 = jnp.bfloat16


def nt(a, b):
    return lax.dot_general(a, b, (((1,), (1,)), ((), ())), preferred_element_type=F32)


def nn(a, b):
    return lax.dot_general(a, b, (((1,), (0,)), ((), ())), preferred_element_type=F32)


def kernel(
    cq, ck, cv, oq, ok, ov, seg, w,
    ctx_out, opt_out,
    cq_v, kk, vv, oq_v, ok_v, ov_v, seg_v, w_v, co_v,
    sx, sxs, rx, rxs, sz, szs, rz, rzs, att, hs, hr,
    in_sem, out_sem, sx_sem, rx_sem, sz_sem, rz_sem,
    gzs_sem, gzr_sem, gxs_sem, gxr_sem, hs_sem, hr_sem, as_sem, ar_sem,
):
    c = lax.axis_index("ctx")
    h = lax.axis_index("head")
    z, g = c // 8, c % 8
    x, core = g // 2, g % 2
    zh, y = h // 4, h % 4
    zo = 3 + core

    def at_ctx(cc):
        return {"ctx": cc, "head": h}

    def x_peer(dx, dc):
        return z * 8 + ((x + dx) % 4) * 2 + (core + dc) % 2

    def head_peer(kz, ky):
        return ((zh + kz) % 2) * 4 + (y + ky) % 4

    barrier = pltpu.get_barrier_semaphore()
    for slot in range(1, 8):
        pl.semaphore_signal(barrier, inc=1, device_id=at_ctx(x_peer(slot // 2, slot % 2)), device_id_type=MESH)
    for k in range(1, NZ):
        pl.semaphore_signal(barrier, inc=1, device_id=at_ctx(((z + k) % NZ) * 8 + g), device_id_type=MESH)
    for k in range(1, 8):
        pl.semaphore_signal(barrier, inc=1, device_id={"ctx": c, "head": head_peer(k // 4, k % 4)}, device_id_type=MESH)

    own = pl.ds(BLOCK, BLOCK)
    anchor = pl.ds(0, BLOCK)
    loads = [
        pltpu.make_async_copy(ck, kk.at[own], in_sem.at[0]),
        pltpu.make_async_copy(oq, oq_v, in_sem.at[1]),
        pltpu.make_async_copy(cv, vv.at[own], in_sem.at[2]),
        pltpu.make_async_copy(ok, ok_v, in_sem.at[3]),
        pltpu.make_async_copy(ov, ov_v, in_sem.at[4]),
        pltpu.make_async_copy(seg, seg_v, in_sem.at[5]),
        pltpu.make_async_copy(w, w_v, in_sem.at[6]),
        pltpu.make_async_copy(cq, cq_v, in_sem.at[7]),
    ]
    for load in loads:
        load.start()
    root_loads = [
        pltpu.make_async_copy(ck, kk.at[anchor], in_sem.at[8]),
        pltpu.make_async_copy(cv, vv.at[anchor], in_sem.at[9]),
    ]

    @pl.when(c == 0)
    def _():
        for load in root_loads:
            load.start()

    def anchor_copies(n, target):
        return [
            pltpu.make_async_remote_copy(
                src_ref=ref.at[anchor], dst_ref=ref.at[anchor],
                send_sem=as_sem.at[n, i], recv_sem=ar_sem.at[i],
                device_id=at_ctx(target), device_id_type=MESH,
            )
            for i, ref in enumerate((kk, vv))
        ]

    def anchor_wait():
        for copy in anchor_copies(0, c):
            copy.wait_recv()

    def anchor_send(n, target):
        for copy in anchor_copies(n, target):
            copy.start()

    def anchor_sent(n):
        for copy in anchor_copies(n, c):
            copy.wait_send()

    passes_on = (g == 0) & ((z == 1) | (z == 2) | (z == 4) | (z == 5) | (z == 6))
    spreads_late = (g == 0) & (z == 3)

    def spread():
        anchor_send(2, z * 8 + 4)
        anchor_send(3, z * 8 + 2)
        anchor_send(4, z * 8 + 6)
        anchor_send(5, z * 8 + 1)

    loads[0].wait()
    loads[1].wait()
    loads[2].wait()
    k_own = kk[own, :]
    vt_own = vv[own, :].astype(F32).T.astype(BF16)

    def partial(q, keys, vt, mask=None):
        s = nt(keys, q) * SCALE
        if mask is not None:
            s = jnp.where(mask, s, FAR)
        m = jnp.max(s, axis=0, keepdims=True)
        p = jnp.exp(s - m)
        if mask is not None:
            p = jnp.where(mask, p, 0.0)
        return m, jnp.sum(p, axis=0, keepdims=True), nn(vt, p.astype(BF16))

    def x_copies(slot, target):
        return [
            pltpu.make_async_remote_copy(
                src_ref=a.at[slot], dst_ref=b.at[slot],
                send_sem=sx_sem.at[i, slot], recv_sem=rx_sem.at[i, slot],
                device_id=at_ctx(target), device_id_type=MESH,
            )
            for i, (a, b) in enumerate(((sx, rx), (sxs, rxs)))
        ]

    def option_head(slot):
        dx, dc = slot // 2, slot % 2
        gd = ((x + dx) % 4) * 2 + (core + dc) % 2
        q = oq_v[:, pl.ds(pl.multiple_of(gd * HEAD, HEAD), HEAD)]
        m, l, mix = partial(q, k_own, vt_own)
        sx[slot] = mix.astype(BF16)
        sxs[slot, 0:1, :] = m
        sxs[slot, 1:2, :] = l

    order = (4, 5, 2, 3, 6, 7, 1, 0)
    option_head(4)
    option_head(5)
    pl.semaphore_wait(barrier, 21)

    @pl.when(c == 0)
    def _():
        for load in root_loads:
            load.wait()
        anchor_send(0, 4 * 8)
        anchor_send(1, 8)

    for pos, slot in enumerate(order):
        if pos >= 2:
            option_head(slot)
        if slot:
            for copy in x_copies(slot, x_peer(slot // 2, slot % 2)):
                copy.start()

    loads[3].wait()
    loads[4].wait()
    loads[5].wait()
    seg_row = jnp.broadcast_to(seg_v[...].astype(F32), (ROWS, ROWS))
    seg_col = seg_row.T
    key_at = lax.broadcasted_iota(jnp.int32, (ROWS, ROWS), 0)
    row_at = lax.broadcasted_iota(jnp.int32, (ROWS, ROWS), 1)
    visible = (seg_row == seg_col) & (row_at >= key_at)
    q_own = oq_v[:, pl.ds(pl.multiple_of(g * HEAD, HEAD), HEAD)]
    vt_self = ov_v[...].astype(F32).T.astype(BF16)
    self_part = partial(q_own, ok_v[...], vt_self, visible)

    for slot in range(1, 8):
        for copy in x_copies(slot, c):
            copy.wait_recv()

    def join(parts):
        top = functools.reduce(jnp.maximum, [m for m, _, _ in parts])
        factors = [jnp.exp(m - top) for m, _, _ in parts]
        total = sum(f * l for f, (_, l, _) in zip(factors, parts))
        mix = sum(f * a for f, (_, _, a) in zip(factors, parts))
        return top, total, mix

    parts = [(sxs[0, 0:1, :], sxs[0, 1:2, :], sx[0].astype(F32))]
    parts += [(rxs[s, 0:1, :], rxs[s, 1:2, :], rx[s].astype(F32)) for s in range(1, 8)]
    top, total, mix = join(parts)

    def z_copies(k, target):
        return [
            pltpu.make_async_remote_copy(
                src_ref=a, dst_ref=b.at[k], send_sem=sz_sem.at[i], recv_sem=rz_sem.at[i, k],
                device_id=at_ctx(target), device_id_type=MESH,
            )
            for i, (a, b) in enumerate(((sz, rz), (szs, rzs)))
        ]

    def gz_copy(k, target):
        return pltpu.make_async_remote_copy(
            src_ref=att.at[g], dst_ref=att.at[g], send_sem=gzs_sem.at[k], recv_sem=gzr_sem,
            device_id=at_ctx(target), device_id_type=MESH,
        )

    @pl.when(z != zo)
    def _():
        sz[...] = mix.astype(BF16)
        szs[0:1, :] = top
        szs[1:2, :] = total
        for copy in z_copies((z - zo + NZ) % NZ, zo * 8 + g):
            copy.start()

    @pl.when((g == 0) & (z > 0) & (z != 3))
    def _():
        anchor_wait()

        @pl.when(z < 7)
        def _():
            anchor_send(0, (z + 1) * 8)

        spread()

    @pl.when(c == 0)
    def _():
        spread()

    @pl.when(z == zo)
    def _():
        for k in range(1, NZ):
            for copy in z_copies(k, c):
                copy.wait_recv()
        all_parts = [(top, total, mix), self_part]
        all_parts += [(rzs[k, 0:1, :], rzs[k, 1:2, :], rz[k].astype(F32)) for k in range(1, NZ)]
        _, whole, summed = join(all_parts)
        att[g] = (summed / whole).T.astype(BF16)
        for k in (4, 5, 3, 6, 2, 7, 1):
            gz_copy(k, ((z + k) % NZ) * 8 + g).start()

    @pl.when(z != zo)
    def _():
        gz_copy(0, c).wait_recv()

    def gx_copy(slot, target):
        return pltpu.make_async_remote_copy(
            src_ref=att.at[g], dst_ref=att.at[g], send_sem=gxs_sem.at[slot], recv_sem=gxr_sem.at[slot],
            device_id=at_ctx(target), device_id_type=MESH,
        )

    for slot in (4, 5, 2, 3, 6, 7, 1):
        gx_copy(slot, x_peer(slot // 2, slot % 2)).start()

    @pl.when(spreads_late)
    def _():
        anchor_wait()
        spread()

    @pl.when((core == 0) & (g > 0))
    def _():
        anchor_wait()
        anchor_send(5, c + 1)

    loads[6].wait()
    loads[7].wait()
    for slot in range(1, 8):
        gx_copy(slot, c).wait_recv()

    projected = nn(att[0], w_v[0:HEAD, :])
    for j in range(1, GROUPS):
        projected = projected + nn(att[j], w_v[j * HEAD : (j + 1) * HEAD, :])
    hs[...] = projected.astype(BF16).reshape(8, 16, HEAD)

    def h_copy(slot, source, target):
        return pltpu.make_async_remote_copy(
            src_ref=hs.at[source], dst_ref=hr.at[slot], send_sem=hs_sem.at[slot], recv_sem=hr_sem.at[slot],
            device_id={"ctx": c, "head": target}, device_id_type=MESH,
        )

    for slot in (6, 5, 7, 4, 2, 1, 3):
        peer = head_peer(slot // 4, slot % 4)
        h_copy(slot, peer, peer).start()

    @pl.when(core == 1)
    def _():
        anchor_wait()

    off = jnp.where(c > 0, 0.0, FAR).astype(F32)
    k_all = kk[...]
    v_all = jnp.concatenate([vv[...], jnp.ones((2 * BLOCK, HEAD), BF16)], axis=1)
    tri = lax.broadcasted_iota(jnp.int32, (ROWS, ROWS), 0) >= lax.broadcasted_iota(jnp.int32, (ROWS, ROWS), 1)
    writes = []
    for j in range(GROUPS):
        for half in range(2):
            r0 = half * ROWS
            seen = BLOCK + r0 + ROWS
            q = cq_v[r0 : r0 + ROWS, j * HEAD : (j + 1) * HEAD]
            s = nt(q, k_all[:seen]) * SCALE
            pieces = [s[:, :BLOCK] + off]
            if half:
                pieces.append(s[:, BLOCK : BLOCK + ROWS])
            pieces.append(jnp.where(tri, s[:, seen - ROWS :], FAR))
            s = jnp.concatenate(pieces, axis=1)
            m = jnp.max(s, axis=1, keepdims=True)
            p = jnp.exp(s - m).astype(BF16)
            r = nn(p, v_all[:seen])
            co_v[r0 : r0 + ROWS, j * HEAD : (j + 1) * HEAD] = (r[:, :HEAD] / r[:, HEAD:]).astype(BF16)
        if j % 2:
            cols = slice((j - 1) * HEAD, (j + 1) * HEAD)
            copy = pltpu.make_async_copy(co_v.at[:, cols], ctx_out.at[:, cols], out_sem.at[j // 2])
            copy.start()
            writes.append(copy)

    for slot in range(1, 8):
        h_copy(slot, 0, h).wait_recv()
    result = hs[h].astype(F32)
    for slot in range(1, 8):
        result = result + hr[slot].astype(F32)
    opt_out[...] = result.astype(BF16)

    for copy in writes:
        copy.wait()
    for slot in range(1, 8):
        for copy in x_copies(slot, c):
            copy.wait_send()
        gx_copy(slot, c).wait_send()
        h_copy(slot, 0, h).wait_send()

    @pl.when(z != zo)
    def _():
        for copy in z_copies(0, c):
            copy.wait_send()

    @pl.when(z == zo)
    def _():
        for k in range(1, NZ):
            gz_copy(k, c).wait_send()

    @pl.when(c == 0)
    def _():
        anchor_sent(0)
        anchor_sent(1)

    @pl.when(passes_on)
    def _():
        anchor_sent(0)

    @pl.when(g == 0)
    def _():
        for n in range(2, 6):
            anchor_sent(n)

    @pl.when((core == 0) & (g > 0))
    def _():
        anchor_sent(5)


def layer(cq, ck, cv, oq, ok, ov, seg, w):
    vmem, dma = pltpu.VMEM, pltpu.SemaphoreType.DMA
    anywhere = pl.BlockSpec(memory_space=pl.ANY)
    return pl.pallas_call(
        kernel,
        name="star_attention",
        out_shape=(
            jax.ShapeDtypeStruct((BLOCK, GROUPS * HEAD), BF16),
            jax.ShapeDtypeStruct((ROWS // 8, HEAD), BF16),
        ),
        in_specs=[anywhere] * 8,
        out_specs=(anywhere, pl.BlockSpec(memory_space=vmem)),
        scratch_shapes=[
            vmem((BLOCK, GROUPS * HEAD), BF16),
            vmem((2 * BLOCK, HEAD), BF16),
            vmem((2 * BLOCK, HEAD), BF16),
            vmem((ROWS, GROUPS * HEAD), BF16),
            vmem((ROWS, HEAD), BF16),
            vmem((ROWS, HEAD), BF16),
            vmem((1, ROWS), jnp.int32),
            vmem((GROUPS * HEAD, HEAD), BF16),
            vmem((BLOCK, GROUPS * HEAD), BF16),
            vmem((8, HEAD, ROWS), BF16),
            vmem((8, 2, ROWS), F32),
            vmem((8, HEAD, ROWS), BF16),
            vmem((8, 2, ROWS), F32),
            vmem((HEAD, ROWS), BF16),
            vmem((2, ROWS), F32),
            vmem((8, HEAD, ROWS), BF16),
            vmem((8, 2, ROWS), F32),
            vmem((8, ROWS, HEAD), BF16),
            vmem((8, 16, HEAD), BF16),
            vmem((8, 16, HEAD), BF16),
            dma((10,)),
            dma((4,)),
            dma((2, 8)),
            dma((2, 8)),
            dma((2,)),
            dma((2, 8)),
            dma((8,)),
            dma(()),
            dma((8,)),
            dma((8,)),
            dma((8,)),
            dma((8,)),
            dma((6, 2)),
            dma((2,)),
        ],
        compiler_params=pltpu.CompilerParams(collective_id=0, has_side_effects=True),
    )(cq, ck, cv, oq, ok, ov, seg.reshape(1, ROWS), w)


def solution(mesh):
    placed = (
        P("ctx", "head"),
        P("ctx", "head"),
        P("ctx", "head"),
        P(None, "head"),
        P(None, "head"),
        P(None, "head"),
        P(),
        P("head", "ctx"),
    )
    return jax.shard_map(
        layer,
        mesh=mesh,
        in_specs=placed,
        out_specs=(P("ctx", "head"), P("head", "ctx")),
        check_vma=False,
    )
```

time: 197 us -> 47.8 us (0.24)
  waiting for transfers between devices: 128 us -> 0 us
  Pallas kernels: 0 us -> 44.5 us
  starting transfers between devices: 38.3 us -> 0 us
  between operations: 14.3 us -> 0.65 us
  matrix products: 6.67 us -> 0 us
  other arithmetic: 5.55 us -> 0 us
    all_to_all x4 -> x0, waiting for transfers between devices: 118 us -> none  [the longest x1 60.5 us: sum_at_owner(): lax.all_to_all(parts, axis, split_axis=0, concat_axis=0, tiled=True)]
    pallas_call x0 -> x1, Pallas kernels: none -> 44.5 us  [layer(): pl.pallas_call(kernel, name='star_attention', out_shape=(jax.ShapeDtypeSt...]
    all_to_all x4 -> x0, starting transfers between devices: 38.2 us -> none  [the longest x2 23.6 us: from_everyone(): lax.all_to_all(jnp.broadcast_to(x[None], (count, *x.shape)), axis, 0, 0,...]
    all_gather x1 -> x0, waiting for transfers between devices: 9.58 us -> none  [from_root(): lax.all_gather(x, axis)]
    dot_general x9 -> x0, matrix products: 6.67 us -> none  [the longest x1 1.47 us: shards(): jnp.einsum('tkgs,skd->tkgd', anchor_probs.astype(jnp.bfloat16), values_an...]
    reduce_sum x5 -> x0, other arithmetic: 2.04 us -> none  [the longest x1 0.74 us: shards(): row_sum = jnp.sum(own_probs, axis=-1) + jnp.sum(anchor_probs, axis=-1)]
  transfers between devices with their start and end apart: 5 -> 0, of which waited for: 5 -> 0; matrix products, arithmetic and copies ran while one was open for 5% -> 0% of each run, Pallas kernels for 0% -> 0%
where the time goes in v1:
time: 47.8 us; the launch traced here: 47.6 us
  Pallas kernels  44.5 us (93%)
  local copies, waits for them, and re-layouts  2.47 us (5%)
  between operations  0.65 us (1%)
    pallas_call x1, Pallas kernels, layer(): pl.pallas_call(kernel, name='star_attention', out_shape=(jax.ShapeDtypeSt...  44.5 us
    unnamed x4, local copies, waits for them, and re-layouts  2.47 us

profile of v1, /device:TPU:1, one launch (start us, length us, event | category | flops | bytes accessed | tf_op | source)
XLA Modules:
  0.0 47.6 jit_solution(12666970053377429356)
XLA Ops:
  0.6 44.5 %star_attention.1 = (bf16[256,1024]{1,0:T(8,128)(2,1)}, bf16[16,128]{1,0:T(8,128)(2,1)}) custom-call(bf16[256,1024]{1,0:T(8,128)(2,1)} %cq.1, bf16[256,128]{1,0:T(8,128)(2,1)} %ck.1, bf16[256,128]{1,0:T(8,128)(2,1)} %cv.1, bf16[128,1024]{1,0:T(8,128)(2,1)} %oq.1, bf16[128,128]{1,0:T(8,128)(2,1)} %ok.1, bf16[128,128]{1,0:T(8,128)(2,1)} %ov.1, ...), custom_call_target="tpu_custom_call" | custom-call | tf_op jit(solution)/shard_map/star_attention/pallas_call | solution.py:367
  45.1 0.0 copy-start
  45.1 1.9 %copy.12 = bf16[256,1024]{1,0:T(8,128)(2,1)} copy(bf16[256,1024]{1,0:T(8,128)(2,1)} %get-tuple-element.4) | data formatting | bytes 1048576
  47.0 0.0 copy-done
  47.0 0.6 %copy.13 = bf16[16,128]{1,0:T(8,128)(2,1)} copy(bf16[16,128]{1,0:T(8,128)(2,1)S(1)} %copy-done) | data formatting | bytes 8192
Async XLA Ops:
  45.1 1.9 %copy-start = (bf16[16,128]{1,0:T(8,128)(2,1)S(1)}, bf16[16,128]{1,0:T(8,128)(2,1)}, u32[]{:S(2)}) copy-start(bf16[16,128]{1,0:T(8,128)(2,1)} %get-tuple-element.5) | copy-start | bytes 12292

commit v2 on v1

--- a/solution.py
+++ b/solution.py
@@ -29,11 +29,11 @@
 
 def kernel(
     cq, ck, cv, oq, ok, ov, seg, w,
-    ctx_out, opt_out,
-    cq_v, kk, vv, oq_v, ok_v, ov_v, seg_v, w_v, co_v,
+    co_v, opt_out,
+    cq_v, kk, vv, oq_v, ok_v, ov_v, seg_v, w_v,
     sx, sxs, rx, rxs, sz, szs, rz, rzs, att, hs, hr,
-    in_sem, out_sem, sx_sem, rx_sem, sz_sem, rz_sem,
-    gzs_sem, gzr_sem, gxs_sem, gxr_sem, hs_sem, hr_sem, as_sem, ar_sem,
+    in_sem, sx_sem, rx_sem, sz_sem, rz_sem,
+    gzs_sem, gzr_sem, gxs_sem, gxr_sem, hs_sem, hr_sem, as_sem, ar_sem, near_sem,
 ):
     c = lax.axis_index("ctx")
     h = lax.axis_index("head")
@@ -51,13 +51,12 @@
     def head_peer(kz, ky):
         return ((zh + kz) % 2) * 4 + (y + ky) % 4
 
-    barrier = pltpu.get_barrier_semaphore()
-    for slot in range(1, 8):
-        pl.semaphore_signal(barrier, inc=1, device_id=at_ctx(x_peer(slot // 2, slot % 2)), device_id_type=MESH)
-    for k in range(1, NZ):
-        pl.semaphore_signal(barrier, inc=1, device_id=at_ctx(((z + k) % NZ) * 8 + g), device_id_type=MESH)
-    for k in range(1, 8):
-        pl.semaphore_signal(barrier, inc=1, device_id={"ctx": c, "head": head_peer(k // 4, k % 4)}, device_id_type=MESH)
+    def along_z(k):
+        zz = (zh * NZ + z + k) % (2 * NZ)
+        return {"ctx": (zz % NZ) * 8 + g, "head": (zz // NZ) * 4 + y}
+
+    def tell(sem, target):
+        pl.semaphore_signal(sem, inc=1, device_id=target, device_id_type=MESH)
 
     own = pl.ds(BLOCK, BLOCK)
     anchor = pl.ds(0, BLOCK)
@@ -71,7 +70,17 @@
         pltpu.make_async_copy(w, w_v, in_sem.at[6]),
         pltpu.make_async_copy(cq, cq_v, in_sem.at[7]),
     ]
-    for load in loads:
+    for load in loads[:3]:
+        load.start()
+
+    barrier = pltpu.get_barrier_semaphore()
+    for slot in range(1, 8):
+        tell(barrier, at_ctx(x_peer(slot // 2, slot % 2)))
+    for k in (1, 15):
+        tell(barrier, along_z(k))
+    for k in range(1, 4):
+        tell(barrier, {"ctx": c, "head": head_peer(0, k)})
+    for load in loads[3:]:
         load.start()
     root_loads = [
         pltpu.make_async_copy(ck, kk.at[anchor], in_sem.at[8]),
@@ -83,36 +92,34 @@
         for load in root_loads:
             load.start()
 
-    def anchor_copies(n, target):
-        return [
-            pltpu.make_async_remote_copy(
-                src_ref=ref.at[anchor], dst_ref=ref.at[anchor],
-                send_sem=as_sem.at[n, i], recv_sem=ar_sem.at[i],
-                device_id=at_ctx(target), device_id_type=MESH,
-            )
-            for i, ref in enumerate((kk, vv))
-        ]
-
-    def anchor_wait():
-        for copy in anchor_copies(0, c):
-            copy.wait_recv()
-
-    def anchor_send(n, target):
-        for copy in anchor_copies(n, target):
-            copy.start()
+    def anchor_copy(i, n, target):
+        ref = (kk, vv)[i]
+        return pltpu.make_async_remote_copy(
+            src_ref=ref.at[anchor], dst_ref=ref.at[anchor],
+            send_sem=as_sem.at[n, i], recv_sem=ar_sem.at[i],
+            device_id=at_ctx(target), device_id_type=MESH,
+        )
+
+    def anchor_wait(i):
+        anchor_copy(i, 0, c).wait_recv()
 
     def anchor_sent(n):
-        for copy in anchor_copies(n, c):
-            copy.wait_send()
-
-    passes_on = (g == 0) & ((z == 1) | (z == 2) | (z == 4) | (z == 5) | (z == 6))
-    spreads_late = (g == 0) & (z == 3)
-
-    def spread():
-        anchor_send(2, z * 8 + 4)
-        anchor_send(3, z * 8 + 2)
-        anchor_send(4, z * 8 + 6)
-        anchor_send(5, z * 8 + 1)
+        for i in range(2):
+            anchor_copy(i, n, c).wait_send()
+
+    def spread(i):
+        for n, gg in ((2, 4), (3, 2), (4, 6), (5, 1)):
+            anchor_copy(i, n, z * 8 + gg).start()
+
+    def relay():
+        for i in range(2):
+            anchor_wait(i)
+
+            @pl.when((z != 3) & (z != 7))
+            def _():
+                anchor_copy(i, 0, (z + 1) * 8).start()
+
+            spread(i)
 
     loads[0].wait()
     loads[1].wait()
@@ -140,33 +147,41 @@
             for i, (a, b) in enumerate(((sx, rx), (sxs, rxs)))
         ]
 
-    def option_head(slot):
-        dx, dc = slot // 2, slot % 2
-        gd = ((x + dx) % 4) * 2 + (core + dc) % 2
-        q = oq_v[:, pl.ds(pl.multiple_of(gd * HEAD, HEAD), HEAD)]
-        m, l, mix = partial(q, k_own, vt_own)
-        sx[slot] = mix.astype(BF16)
-        sxs[slot, 0:1, :] = m
-        sxs[slot, 1:2, :] = l
-
-    order = (4, 5, 2, 3, 6, 7, 1, 0)
-    option_head(4)
-    option_head(5)
-    pl.semaphore_wait(barrier, 21)
+    def option_heads(slots):
+        qs = []
+        for slot in slots:
+            gd = ((x + slot // 2) % 4) * 2 + (core + slot % 2) % 2
+            qs.append(oq_v[:, pl.ds(pl.multiple_of(gd * HEAD, HEAD), HEAD)])
+        m, l, mix = partial(jnp.concatenate(qs, axis=0), k_own, vt_own)
+        for n, slot in enumerate(slots):
+            lanes = slice(n * ROWS, (n + 1) * ROWS)
+            sx[slot] = mix[:, lanes].astype(BF16)
+            sxs[slot, 0:1, :] = m[:, lanes]
+            sxs[slot, 1:2, :] = l[:, lanes]
+
+    def send_heads(slots):
+        for slot in slots:
+            if slot:
+                for copy in x_copies(slot, x_peer(slot // 2, slot % 2)):
+                    copy.start()
+
+    option_heads((4, 5, 2, 3))
+    pl.semaphore_wait(barrier, 12)
+    send_heads((4, 5, 2, 3))
+    for k in (1, 15):
+        tell(near_sem.at[0], along_z(k))
 
     @pl.when(c == 0)
     def _():
-        for load in root_loads:
-            load.wait()
-        anchor_send(0, 4 * 8)
-        anchor_send(1, 8)
-
-    for pos, slot in enumerate(order):
-        if pos >= 2:
-            option_head(slot)
-        if slot:
-            for copy in x_copies(slot, x_peer(slot // 2, slot % 2)):
-                copy.start()
+        for i in range(2):
+            root_loads[i].wait()
+            anchor_copy(i, 1, 8).start()
+
+    option_heads((6, 7, 1, 0))
+    send_heads((6, 7, 1))
+    pl.semaphore_wait(near_sem.at[0], 2)
+    for k in (2, 14):
+        tell(near_sem.at[1], along_z(k))
 
     loads[3].wait()
     loads[4].wait()
@@ -180,6 +195,15 @@
     vt_self = ov_v[...].astype(F32).T.astype(BF16)
     self_part = partial(q_own, ok_v[...], vt_self, visible)
 
+    pl.semaphore_wait(near_sem.at[1], 2)
+    for k in (4, 12):
+        tell(near_sem.at[2], along_z(k))
+
+    @pl.when(c == 0)
+    def _():
+        for i in range(2):
+            anchor_copy(i, 0, 4 * 8).start()
+
     for slot in range(1, 8):
         for copy in x_copies(slot, c):
             copy.wait_recv()
@@ -218,19 +242,18 @@
         for copy in z_copies((z - zo + NZ) % NZ, zo * 8 + g):
             copy.start()
 
-    @pl.when((g == 0) & (z > 0) & (z != 3))
-    def _():
-        anchor_wait()
-
-        @pl.when(z < 7)
-        def _():
-            anchor_send(0, (z + 1) * 8)
-
-        spread()
+    @pl.when((g == 0) & ((z == 1) | (z == 2) | (z == 4) | (z == 5)))
+    def _():
+        relay()
 
     @pl.when(c == 0)
     def _():
-        spread()
+        for i in range(2):
+            spread(i)
+
+    pl.semaphore_wait(near_sem.at[2], 2)
+    for k in (1, 15):
+        tell(near_sem.at[3], along_z(k))
 
     @pl.when(z == zo)
     def _():
@@ -257,16 +280,11 @@
     for slot in (4, 5, 2, 3, 6, 7, 1):
         gx_copy(slot, x_peer(slot // 2, slot % 2)).start()
 
-    @pl.when(spreads_late)
-    def _():
-        anchor_wait()
-        spread()
-
-    @pl.when((core == 0) & (g > 0))
-    def _():
-        anchor_wait()
-        anchor_send(5, c + 1)
-
+    @pl.when((g == 0) & ((z == 3) | (z == 6)))
+    def _():
+        relay()
+
+    pl.semaphore_wait(near_sem.at[3], 2)
     loads[6].wait()
     loads[7].wait()
     for slot in range(1, 8):
@@ -287,15 +305,25 @@
         peer = head_peer(slot // 4, slot % 4)
         h_copy(slot, peer, peer).start()
 
+    @pl.when((g == 0) & (z == 7))
+    def _():
+        relay()
+
+    @pl.when((core == 0) & (g > 0))
+    def _():
+        for i in range(2):
+            anchor_wait(i)
+            anchor_copy(i, 5, c + 1).start()
+
     @pl.when(core == 1)
     def _():
-        anchor_wait()
+        for i in range(2):
+            anchor_wait(i)
 
     off = jnp.where(c > 0, 0.0, FAR).astype(F32)
     k_all = kk[...]
     v_all = jnp.concatenate([vv[...], jnp.ones((2 * BLOCK, HEAD), BF16)], axis=1)
     tri = lax.broadcasted_iota(jnp.int32, (ROWS, ROWS), 0) >= lax.broadcasted_iota(jnp.int32, (ROWS, ROWS), 1)
-    writes = []
     for j in range(GROUPS):
         for half in range(2):
             r0 = half * ROWS
@@ -311,11 +339,6 @@
             p = jnp.exp(s - m).astype(BF16)
             r = nn(p, v_all[:seen])
             co_v[r0 : r0 + ROWS, j * HEAD : (j + 1) * HEAD] = (r[:, :HEAD] / r[:, HEAD:]).astype(BF16)
-        if j % 2:
-            cols = slice((j - 1) * HEAD, (j + 1) * HEAD)
-            copy = pltpu.make_async_copy(co_v.at[:, cols], ctx_out.at[:, cols], out_sem.at[j // 2])
-            copy.start()
-            writes.append(copy)
 
     for slot in range(1, 8):
         h_copy(slot, 0, h).wait_recv()
@@ -324,8 +347,6 @@
         result = result + hr[slot].astype(F32)
     opt_out[...] = result.astype(BF16)
 
-    for copy in writes:
-        copy.wait()
     for slot in range(1, 8):
         for copy in x_copies(slot, c):
             copy.wait_send()
@@ -347,7 +368,7 @@
         anchor_sent(0)
         anchor_sent(1)
 
-    @pl.when(passes_on)
+    @pl.when((g == 0) & (z > 0) & (z != 3) & (z != 7))
     def _():
         anchor_sent(0)
 
@@ -359,20 +380,25 @@
     @pl.when((core == 0) & (g > 0))
     def _():
         anchor_sent(5)
+
+
+def put_out(co, oo, ctx_out, opt_out, sem):
+    copies = [pltpu.make_async_copy(co, ctx_out, sem.at[0]), pltpu.make_async_copy(oo, opt_out, sem.at[1])]
+    for copy in copies:
+        copy.start()
+    for copy in copies:
+        copy.wait()
 
 
 def layer(cq, ck, cv, oq, ok, ov, seg, w):
     vmem, dma = pltpu.VMEM, pltpu.SemaphoreType.DMA
     anywhere = pl.BlockSpec(memory_space=pl.ANY)
-    return pl.pallas_call(
+    parts = pl.pallas_call(
         kernel,
         name="star_attention",
-        out_shape=(
-            jax.ShapeDtypeStruct((BLOCK, GROUPS * HEAD), BF16),
-            jax.ShapeDtypeStruct((ROWS // 8, HEAD), BF16),
-        ),
+        out_shape=(vmem((BLOCK, GROUPS * HEAD), BF16), vmem((ROWS // 8, HEAD), BF16)),
         in_specs=[anywhere] * 8,
-        out_specs=(anywhere, pl.BlockSpec(memory_space=vmem)),
+        out_specs=(pl.BlockSpec(memory_space=vmem), pl.BlockSpec(memory_space=vmem)),
         scratch_shapes=[
             vmem((BLOCK, GROUPS * HEAD), BF16),
             vmem((2 * BLOCK, HEAD), BF16),
@@ -382,7 +408,6 @@
             vmem((ROWS, HEAD), BF16),
             vmem((1, ROWS), jnp.int32),
             vmem((GROUPS * HEAD, HEAD), BF16),
-            vmem((BLOCK, GROUPS * HEAD), BF16),
             vmem((8, HEAD, ROWS), BF16),
             vmem((8, 2, ROWS), F32),
             vmem((8, HEAD, ROWS), BF16),
@@ -395,7 +420,6 @@
             vmem((8, 16, HEAD), BF16),
             vmem((8, 16, HEAD), BF16),
             dma((10,)),
-            dma((4,)),
             dma((2, 8)),
             dma((2, 8)),
             dma((2,)),
@@ -408,9 +432,21 @@
             dma((8,)),
             dma((6, 2)),
             dma((2,)),
+            pltpu.SemaphoreType.REGULAR((4,)),
         ],
         compiler_params=pltpu.CompilerParams(collective_id=0, has_side_effects=True),
     )(cq, ck, cv, oq, ok, ov, seg.reshape(1, ROWS), w)
+    return pl.pallas_call(
+        put_out,
+        name="put_out",
+        out_shape=(
+            jax.ShapeDtypeStruct((BLOCK, GROUPS * HEAD), BF16),
+            jax.ShapeDtypeStruct((ROWS // 8, HEAD), BF16),
+        ),
+        in_specs=[pl.BlockSpec(memory_space=vmem)] * 2,
+        out_specs=(anywhere, anywhere),
+        scratch_shapes=[dma((2,))],
+    )(*[pltpu.with_memory_space_constraint(part, vmem) for part in parts])
 
 
 def solution(mesh):

time: 47.8 us -> 43.7 us (0.914)
  local copies, waits for them, and re-layouts: 2.47 us -> 0 us
  Pallas kernels: 44.5 us -> 42.9 us
    unnamed x4 -> x0, local copies, waits for them, and re-layouts: 2.47 us -> none
    pallas_call x1 -> x2, Pallas kernels: 44.5 us -> 42.9 us  [the longest x1 42.1 us: layer(): pl.pallas_call(kernel, name='star_attention', out_shape=(vmem((BLOCK, GRO...]
where the time goes in v2:
time: 43.7 us; the launch traced here: 43.6 us
  Pallas kernels  42.9 us (98%)
  between operations  0.64 us (1%)
    pallas_call x1, Pallas kernels, layer(): pl.pallas_call(kernel, name='star_attention', out_shape=(vmem((BLOCK, GRO...  42.1 us

profile of v2, /device:TPU:1, one launch (start us, length us, event | category | flops | bytes accessed | tf_op | source)
XLA Modules:
  0.0 43.6 jit_solution(9290160699073967566)
XLA Ops:
  0.6 42.1 %star_attention.1 = (bf16[256,1024]{1,0:T(8,128)(2,1)S(1)}, bf16[16,128]{1,0:T(8,128)(2,1)S(1)}) custom-call(bf16[256,1024]{1,0:T(8,128)(2,1)} %cq.1, bf16[256,128]{1,0:T(8,128)(2,1)} %ck.1, bf16[256,128]{1,0:T(8,128)(2,1)} %cv.1, bf16[128,1024]{1,0:T(8,128)(2,1)} %oq.1, bf16[128,128]{1,0:T(8,128)(2,1)} %ok.1, bf16[128,128]{1,0:T(8,128)(2,1)} %ov.1, ...), custom_call_target="tpu_custom_call" | custom-call | tf_op jit(solution)/shard_map/star_attention/pallas_call | solution.py:396
  42.8 0.8 %put_out.1 = (bf16[256,1024]{1,0:T(8,128)(2,1)}, bf16[16,128]{1,0:T(8,128)(2,1)}) custom-call(bf16[256,1024]{1,0:T(8,128)(2,1)S(1)} %get-tuple-element.4.co, bf16[16,128]{1,0:T(8,128)(2,1)S(1)} %get-tuple-element.5.oo), custom_call_target="tpu_custom_call" | custom-call | tf_op jit(solution)/shard_map/put_out/pallas_call | solution.py:439

commit v3 on v2

v3 whole, which is shorter than its diff:
```python
import functools

import jax
import jax.numpy as jnp
from jax import lax
from jax.experimental import pallas as pl
from jax.experimental.pallas import tpu as pltpu
from jax.sharding import PartitionSpec as P

MESH = pl.DeviceIdType.MESH
HEAD = 128
ROWS = 128
BLOCK = 256
GROUPS = 8
NZ = 8
OWNER_Z = 3
PIECES = 2
PIECE = HEAD // PIECES
QUARTER = BLOCK // 4
SCALE = HEAD ** (-0.5)
FAR = -1e30
F32 = jnp.float32
BF16 = jnp.bfloat16


def nt(a, b):
    return lax.dot_general(a, b, (((1,), (1,)), ((), ())), preferred_element_type=F32)


def nn(a, b):
    return lax.dot_general(a, b, (((1,), (0,)), ((), ())), preferred_element_type=F32)


def kernel(
    cq, ck, cv, oq, ok, ov, seg, w,
    ctx_out, opt_out,
    cq_v, kv, co_v, oq_v, ok_v, ov_v, seg_v, w_v, wt,
    sx, sxs, rx, rxs, sz, szs, rz, rzs, att, hs, hr,
    in_sem, out_sem, sx_sem, rx_sem, sz_sem, rz_sem,
    gzs_sem, gzr_sem, gxs_sem, gxr_sem, hs_sem, hr_sem, as_sem, ar_sem, near_sem,
):
    c = lax.axis_index("ctx")
    h = lax.axis_index("head")
    z, g = c // 8, c % 8
    x, core = g // 2, g % 2
    zh, y = h // 4, h % 4
    zo = OWNER_Z + core

    def at_ctx(cc):
        return {"ctx": cc, "head": h}

    def x_peer(dx, dc):
        return z * 8 + ((x + dx) % 4) * 2 + (core + dc) % 2

    def head_peer(kz, ky):
        return ((zh + kz) % 2) * 4 + (y + ky) % 4

    def along_z(k):
        zz = (zh * NZ + z + k) % (2 * NZ)
        return {"ctx": (zz % NZ) * 8 + g, "head": (zz // NZ) * 4 + y}

    def tell(sem, target):
        pl.semaphore_signal(sem, inc=1, device_id=target, device_id_type=MESH)

    own = pl.ds(BLOCK, BLOCK)
    anchor = pl.ds(0, BLOCK)
    def arrived(ref, sem):
        pltpu.make_async_copy(ref, ref, sem).wait()

    def query_load(dx):
        cols = pl.ds(pl.multiple_of(((x + dx) % 4) * 2 * HEAD, 2 * HEAD), 2 * HEAD)
        return pltpu.make_async_copy(oq.at[:, cols], oq_v.at[:, cols], in_sem.at[0 if dx in (1, 2) else 1])

    pltpu.make_async_copy(ck, kv.at[0, own], in_sem.at[0]).start()
    for dx in (2, 1):
        query_load(dx).start()
    pltpu.make_async_copy(cv, kv.at[1, own], in_sem.at[0]).start()
    for dx in (3, 0):
        query_load(dx).start()

    barrier = pltpu.get_barrier_semaphore()
    for slot in range(1, 8):
        tell(barrier, at_ctx(x_peer(slot // 2, slot % 2)))
    for k in (1, 15):
        tell(barrier, along_z(k))
    for k in range(1, 4):
        tell(barrier, {"ctx": c, "head": head_peer(0, k)})
    pltpu.make_async_copy(ok, ok_v, in_sem.at[2]).start()
    pltpu.make_async_copy(ov, ov_v, in_sem.at[2]).start()
    pltpu.make_async_copy(seg, seg_v, in_sem.at[3]).start()
    pltpu.make_async_copy(w, w_v, in_sem.at[4]).start()
    pltpu.make_async_copy(cq, cq_v, in_sem.at[5]).start()

    @pl.when(c == 0)
    def _():
        pltpu.make_async_copy(ck, kv.at[0, anchor], in_sem.at[6]).start()
        pltpu.make_async_copy(cv, kv.at[1, anchor], in_sem.at[6]).start()

    def anchor_copy(q, n, target):
        ref = kv.at[:, pl.ds(pl.multiple_of(q * QUARTER, QUARTER), QUARTER)]
        return pltpu.make_async_remote_copy(
            src_ref=ref, dst_ref=ref, send_sem=as_sem.at[n], recv_sem=ar_sem.at[q],
            device_id=at_ctx(target), device_id_type=MESH,
        )

    def anchor_sent(n, quarters):
        arrived(kv.at[:, 0 : quarters * QUARTER], as_sem.at[n])

    arrived(oq_v, in_sem.at[0])
    k_own = kv[0, own, :]
    vt_own = kv[1, own, :].astype(F32).T.astype(BF16)

    def partial(q, keys, vt, mask=None):
        s = nt(keys, q) * SCALE
        if mask is not None:
            s = jnp.where(mask, s, FAR)
        m = jnp.max(s, axis=0, keepdims=True)
        p = jnp.exp(s - m)
        if mask is not None:
            p = jnp.where(mask, p, 0.0)
        return m, jnp.sum(p, axis=0, keepdims=True), nn(vt, p.astype(BF16))

    def x_copy(i, slot, target):
        src, dst = (sxs, rxs) if i == PIECES else (sx.at[i], rx.at[i])
        return pltpu.make_async_remote_copy(
            src_ref=src.at[slot], dst_ref=dst.at[slot],
            send_sem=sx_sem.at[i], recv_sem=rx_sem.at[i],
            device_id=at_ctx(target), device_id_type=MESH,
        )

    others = pl.ds(1, 7)

    def piece(i):
        return slice(i * PIECE, (i + 1) * PIECE)

    def option_heads(slots):
        qs = []
        for slot in slots:
            gd = ((x + slot // 2) % 4) * 2 + (core + slot % 2) % 2
            qs.append(oq_v[:, pl.ds(pl.multiple_of(gd * HEAD, HEAD), HEAD)])
        m, l, mix = partial(jnp.concatenate(qs, axis=0), k_own, vt_own)
        for n, slot in enumerate(slots):
            lanes = slice(n * ROWS, (n + 1) * ROWS)
            for i in range(PIECES):
                sx[i, slot] = mix[piece(i), lanes].astype(BF16)
            sxs[slot, 0:1, :] = m[:, lanes]
            sxs[slot, 1:2, :] = l[:, lanes]

    def send_heads(i, slots):
        for slot in slots:
            x_copy(i, slot, x_peer(slot // 2, slot % 2)).start()

    option_heads((4, 5, 2, 3))
    pl.semaphore_wait(barrier, 12)
    send_heads(PIECES, (4, 5, 2, 3))
    send_heads(0, (4, 5, 2, 3))
    for k in (1, 15):
        tell(near_sem.at[0], along_z(k))

    arrived(oq_v.at[:, 0 : 4 * HEAD], in_sem.at[1])
    option_heads((6, 7, 1, 0))
    send_heads(PIECES, (6, 7, 1))
    send_heads(0, (6, 7, 1))
    for i in range(1, PIECES):
        send_heads(i, (4, 5, 2, 3, 6, 7, 1))

    @pl.when(c == 0)
    def _():
        arrived(kv.at[:, anchor], in_sem.at[6])
        for q in (2, 1, 3):
            anchor_copy(q, 0, q * 2).start()

    pl.semaphore_wait(near_sem.at[0], 2)
    for k in (2, 14):
        tell(near_sem.at[1], along_z(k))

    arrived(kv.at[0, own], in_sem.at[2])
    arrived(seg_v, in_sem.at[3])
    seg_row = jnp.broadcast_to(seg_v[...].astype(F32), (ROWS, ROWS))
    seg_col = seg_row.T
    key_at = lax.broadcasted_iota(jnp.int32, (ROWS, ROWS), 0)
    row_at = lax.broadcasted_iota(jnp.int32, (ROWS, ROWS), 1)
    visible = (seg_row == seg_col) & (row_at >= key_at)
    q_own = oq_v[:, pl.ds(pl.multiple_of(g * HEAD, HEAD), HEAD)]
    vt_self = ov_v[...].astype(F32).T.astype(BF16)
    self_part = partial(q_own, ok_v[...], vt_self, visible)

    arrived(w_v, in_sem.at[4])
    for i in range(PIECES):
        rows = [w_v[j * HEAD + i * PIECE : j * HEAD + (i + 1) * PIECE, :] for j in range(GROUPS)]
        wt[i] = jnp.concatenate(rows, axis=0).astype(F32).T.astype(BF16)

    pl.semaphore_wait(near_sem.at[1], 2)
    for k in (4, 12):
        tell(near_sem.at[2], along_z(k))

    def factors_of(tops):
        top = functools.reduce(jnp.maximum, tops)
        return top, [jnp.exp(m - top) for m in tops]

    def z_copy(i, k, target):
        src, dst = (szs, rzs) if i == PIECES else (sz.at[i], rz.at[i])
        return pltpu.make_async_remote_copy(
            src_ref=src, dst_ref=dst.at[k], send_sem=sz_sem.at[i], recv_sem=rz_sem.at[i],
            device_id=at_ctx(target), device_id_type=MESH,
        )

    to_owner = (z - zo + NZ) % NZ
    owner = zo * 8 + g
    arrived(rxs.at[others], rx_sem.at[PIECES])
    top, factors = factors_of([sxs[0, 0:1, :]] + [rxs[k, 0:1, :] for k in range(1, 8)])
    total = factors[0] * sxs[0, 1:2, :]
    for k in range(1, 8):
        total = total + factors[k] * rxs[k, 1:2, :]

    @pl.when(z != zo)
    def _():
        szs[0:1, :] = top
        szs[1:2, :] = total
        z_copy(PIECES, to_owner, owner).start()

    mixes = []
    for i in range(PIECES):
        arrived(rx.at[i, others], rx_sem.at[i])
        mix = factors[0] * sx[i, 0].astype(F32)
        for k in range(1, 8):
            mix = mix + factors[k] * rx[i, k].astype(F32)
        mixes.append(mix)

        @pl.when(z != zo)
        def _():
            sz[i] = mix.astype(BF16)
            z_copy(i, to_owner, owner).start()

    at_foot = (z == 0) & (core == 0)

    def anchor_up():
        @pl.when(x > 0)
        def _():
            anchor_copy(x, 0, c).wait_recv()

        for k in (7, 6, 5, 4, 3, 2, 1):
            anchor_copy(x, 1, k * 8 + g).start()

    pl.semaphore_wait(near_sem.at[2], 2)
    for k in (1, 15):
        tell(near_sem.at[3], along_z(k))

    @pl.when(at_foot)
    def _():
        anchor_up()

    def gz_copy(i, target):
        return pltpu.make_async_remote_copy(
            src_ref=att.at[i, g], dst_ref=att.at[i, g], send_sem=gzs_sem.at[i], recv_sem=gzr_sem.at[i],
            device_id=at_ctx(target), device_id_type=MESH,
        )

    def gx_copy(i, target):
        return pltpu.make_async_remote_copy(
            src_ref=att.at[i, g], dst_ref=att.at[i, g], send_sem=gxs_sem.at[i], recv_sem=gxr_sem.at[i],
            device_id=at_ctx(target), device_id_type=MESH,
        )

    def gx_send(i):
        for slot in (4, 5, 2, 3, 6, 7, 1):
            gx_copy(i, x_peer(slot // 2, slot % 2)).start()

    @pl.when(z == zo)
    def _():
        self_top, self_total, self_mix = self_part
        arrived(rzs.at[others], rz_sem.at[PIECES])
        _, parts = factors_of([top, self_top] + [rzs[k, 0:1, :] for k in range(1, NZ)])
        whole = parts[0] * total + parts[1] * self_total
        for k in range(1, NZ):
            whole = whole + parts[k + 1] * rzs[k, 1:2, :]
        for i in range(PIECES):
            arrived(rz.at[i, others], rz_sem.at[i])
            summed = parts[0] * mixes[i] + parts[1] * self_mix[piece(i)]
            for k in range(1, NZ):
                summed = summed + parts[k + 1] * rz[i, k].astype(F32)
            att[i, g] = (summed / whole).astype(BF16)
            for k in (5, 4, 6, 7, 1, 2, 3):
                gz_copy(i, ((z + k) % NZ) * 8 + g).start()
        for i in range(PIECES):
            gx_send(i)

    @pl.when(z != zo)
    def _():
        for i in range(PIECES):
            arrived(att.at[i, 0], gzr_sem.at[i])
            gx_send(i)

    pl.semaphore_wait(near_sem.at[3], 2)
    arrived(cq_v, in_sem.at[5])

    projected = None
    for i in range(PIECES):
        arrived(att.at[i, others], gxr_sem.at[i])
        share = nn(wt[i], att[i].reshape(GROUPS * PIECE, ROWS))
        projected = share if projected is None else projected + share
    hs[...] = projected.T.astype(BF16).reshape(8, 16, HEAD)

    def h_copy(slot, source, target):
        return pltpu.make_async_remote_copy(
            src_ref=hs.at[source], dst_ref=hr.at[slot], send_sem=hs_sem, recv_sem=hr_sem,
            device_id={"ctx": c, "head": target}, device_id_type=MESH,
        )

    for slot in (6, 5, 7, 4, 2, 1, 3):
        peer = head_peer(slot // 4, slot % 4)
        h_copy(slot, peer, peer).start()

    @pl.when(core == 0)
    def _():
        @pl.when(z > 0)
        def _():
            anchor_copy(x, 0, c).wait_recv()

        for k in (2, 1, 3):

            @pl.when((z > 0) | ((x + k) % 4 > 0))
            def _():
                anchor_copy(x, 2, z * 8 + ((x + k) % 4) * 2).start()

        anchor_copy(x, 3, c + 1).start()

    @pl.when((core == 0) & (c > 0))
    def _():
        for k in (1, 3, 2):
            q = (x + k) % 4
            anchor_copy(q, 0, c).wait_recv()
            anchor_copy(q, 3, c + 1).start()

    @pl.when(c == 0)
    def _():
        for q in range(1, 4):
            anchor_copy(q, 3, 1).start()

    @pl.when(core == 1)
    def _():
        for q in range(4):
            anchor_copy(q, 0, c).wait_recv()

    off = jnp.where(c > 0, 0.0, FAR).astype(F32)
    k_all = kv[0]
    v_all = jnp.concatenate([kv[1], jnp.ones((2 * BLOCK, HEAD), BF16)], axis=1)
    tri = lax.broadcasted_iota(jnp.int32, (ROWS, ROWS), 0) >= lax.broadcasted_iota(jnp.int32, (ROWS, ROWS), 1)
    for j in range(GROUPS):
        for half in range(2):
            r0 = half * ROWS
            seen = BLOCK + r0 + ROWS
            q = cq_v[r0 : r0 + ROWS, j * HEAD : (j + 1) * HEAD]
            s = nt(q, k_all[:seen]) * SCALE
            pieces = [s[:, :BLOCK] + off]
            if half:
                pieces.append(s[:, BLOCK : BLOCK + ROWS])
            pieces.append(jnp.where(tri, s[:, seen - ROWS :], FAR))
            s = jnp.concatenate(pieces, axis=1)
            m = jnp.max(s, axis=1, keepdims=True)
            p = jnp.exp(s - m).astype(BF16)
            r = nn(p, v_all[:seen])
            co_v[r0 : r0 + ROWS, j * HEAD : (j + 1) * HEAD] = (r[:, :HEAD] / r[:, HEAD:]).astype(BF16)
        if j % 2:
            cols = slice((j - 1) * HEAD, (j + 1) * HEAD)
            pltpu.make_async_copy(co_v.at[:, cols], ctx_out.at[:, cols], out_sem).start()

    arrived(co_v, out_sem)
    arrived(sxs.at[others], sx_sem.at[PIECES])
    arrived(hs.at[others], hs_sem)
    for i in range(PIECES):
        arrived(sx.at[i, others], sx_sem.at[i])
        arrived(att.at[i, others], gxs_sem.at[i])

    @pl.when(z != zo)
    def _():
        arrived(szs, sz_sem.at[PIECES])
        for i in range(PIECES):
            arrived(sz.at[i], sz_sem.at[i])

    @pl.when(z == zo)
    def _():
        for i in range(PIECES):
            arrived(att.at[i, others], gzs_sem.at[i])

    @pl.when(c == 0)
    def _():
        anchor_sent(0, 3)

    @pl.when(at_foot)
    def _():
        anchor_sent(1, 7)

    @pl.when(core == 0)
    def _():
        @pl.when((z == 0) & (x > 0))
        def _():
            anchor_sent(2, 2)

        @pl.when((z > 0) | (x == 0))
        def _():
            anchor_sent(2, 3)

        anchor_sent(3, 4)

    arrived(hr.at[others], hr_sem)
    result = hs[h].astype(F32)
    for slot in range(1, 8):
        result = result + hr[slot].astype(F32)
    opt_out[...] = result.astype(BF16)


def put_out(co, oo, ctx_out, opt_out, sem):
    copies = [pltpu.make_async_copy(oo, opt_out, sem.at[8])]
    for n in range(8):
        rows = pl.ds(n * 32, 32)
        copies.append(pltpu.make_async_copy(co.at[rows], ctx_out.at[rows], sem.at[n]))
    for copy in copies:
        copy.start()
    for copy in copies:
        copy.wait()


def layer(cq, ck, cv, oq, ok, ov, seg, w):
    vmem, dma = pltpu.VMEM, pltpu.SemaphoreType.DMA
    anywhere = pl.BlockSpec(memory_space=pl.ANY)
    parts = pl.pallas_call(
        kernel,
        name="star_attention",
        out_shape=(vmem((BLOCK, GROUPS * HEAD), BF16), vmem((ROWS // 8, HEAD), BF16)),
        in_specs=[anywhere] * 8,
        out_specs=(anywhere, pl.BlockSpec(memory_space=vmem)),
        scratch_shapes=[
            vmem((BLOCK, GROUPS * HEAD), BF16),
            vmem((2, 2 * BLOCK, HEAD), BF16),
            vmem((BLOCK, GROUPS * HEAD), BF16),
            vmem((ROWS, GROUPS * HEAD), BF16),
            vmem((ROWS, HEAD), BF16),
            vmem((ROWS, HEAD), BF16),
            vmem((1, ROWS), jnp.int32),
            vmem((GROUPS * HEAD, HEAD), BF16),
            vmem((PIECES, HEAD, GROUPS * PIECE), BF16),
            vmem((PIECES, 8, PIECE, ROWS), BF16),
            vmem((8, 2, ROWS), F32),
            vmem((PIECES, 8, PIECE, ROWS), BF16),
            vmem((8, 2, ROWS), F32),
            vmem((PIECES, PIECE, ROWS), BF16),
            vmem((2, ROWS), F32),
            vmem((PIECES, 8, PIECE, ROWS), BF16),
            vmem((8, 2, ROWS), F32),
            vmem((PIECES, 8, PIECE, ROWS), BF16),
            vmem((8, 16, HEAD), BF16),
            vmem((8, 16, HEAD), BF16),
            dma((7,)),
            dma(()),
            dma((PIECES + 1,)),
            dma((PIECES + 1,)),
            dma((PIECES + 1,)),
            dma((PIECES + 1,)),
            dma((PIECES,)),
            dma((PIECES,)),
            dma((PIECES,)),
            dma((PIECES,)),
            dma(()),
            dma(()),
            dma((4,)),
            dma((4,)),
            pltpu.SemaphoreType.REGULAR((4,)),
        ],
        compiler_params=pltpu.CompilerParams(collective_id=0, has_side_effects=True),
    )(cq, ck, cv, oq, ok, ov, seg.reshape(1, ROWS), w)
    return pl.pallas_call(
        put_out,
        name="put_out",
        out_shape=(
            jax.ShapeDtypeStruct((BLOCK, GROUPS * HEAD), BF16),
            jax.ShapeDtypeStruct((ROWS // 8, HEAD), BF16),
        ),
        in_specs=[pl.BlockSpec(memory_space=vmem)] * 2,
        out_specs=(anywhere, anywhere),
        scratch_shapes=[dma((9,))],
    )(*[pltpu.with_memory_space_constraint(part, vmem) for part in parts])


def solution(mesh):
    placed = (
        P("ctx", "head"),
        P("ctx", "head"),
        P("ctx", "head"),
        P(None, "head"),
        P(None, "head"),
        P(None, "head"),
        P(),
        P("head", "ctx"),
    )
    return jax.shard_map(
        layer,
        mesh=mesh,
        in_specs=placed,
        out_specs=(P("ctx", "head"), P("head", "ctx")),
        check_vma=False,
    )
```

time: 43.7 us -> 42.3 us (0.968)
  Pallas kernels: 42.9 us -> 41.5 us
    pallas_call x1, Pallas kernels: 42.1 us -> 40.6 us  [layer(): pl.pallas_call(kernel, name='star_attention', out_shape=(vmem((BLOCK, GRO...]
where the time goes in v3:
time: 42.3 us; the launch traced here: 42.1 us
  Pallas kernels  41.5 us (98%)
  between operations  0.64 us (2%)
    pallas_call x1, Pallas kernels, layer(): pl.pallas_call(kernel, name='star_attention', out_shape=(vmem((BLOCK, GRO...  40.6 us
    pallas_call x1, Pallas kernels, layer(): pl.pallas_call(put_out, name='put_out', out_shape=(jax.ShapeDtypeStruct((...  0.86 us

profile of v3, /device:TPU:1, one launch (start us, length us, event | category | flops | bytes accessed | tf_op | source)
XLA Modules:
  0.0 42.1 jit_solution(9072498396991751903)
XLA Ops:
  0.6 40.6 %star_attention.1 = (bf16[256,1024]{1,0:T(8,128)(2,1)S(1)}, bf16[16,128]{1,0:T(8,128)(2,1)S(1)}) custom-call(bf16[256,1024]{1,0:T(8,128)(2,1)} %cq.1, bf16[256,128]{1,0:T(8,128)(2,1)} %ck.1, bf16[256,128]{1,0:T(8,128)(2,1)} %cv.1, bf16[128,1024]{1,0:T(8,128)(2,1)} %oq.1, bf16[128,128]{1,0:T(8,128)(2,1)} %ok.1, bf16[128,128]{1,0:T(8,128)(2,1)} %ov.1, ...), custom_call_target="tpu_custom_call" | custom-call | tf_op jit(solution)/shard_map/star_attention/pallas_call | solution.py:427
  41.3 0.9 %put_out.1 = (bf16[256,1024]{1,0:T(8,128)(2,1)}, bf16[16,128]{1,0:T(8,128)(2,1)}) custom-call(bf16[256,1024]{1,0:T(8,128)(2,1)S(1)} %get-tuple-element.4.co, bf16[16,128]{1,0:T(8,128)(2,1)S(1)} %get-tuple-element.5.oo), custom_call_target="tpu_custom_call" | custom-call | tf_op jit(solution)/shard_map/put_out/pallas_call | solution.py:472

commit v4 on v3

--- a/solution.py
+++ b/solution.py
@@ -35,9 +35,9 @@
     cq, ck, cv, oq, ok, ov, seg, w,
     ctx_out, opt_out,
     cq_v, kv, co_v, oq_v, ok_v, ov_v, seg_v, w_v, wt,
-    sx, sxs, rx, rxs, sz, szs, rz, rzs, att, hs, hr,
-    in_sem, out_sem, sx_sem, rx_sem, sz_sem, rz_sem,
-    gzs_sem, gzr_sem, gxs_sem, gxr_sem, hs_sem, hr_sem, as_sem, ar_sem, near_sem,
+    sx, sxs, px, pxs, rx, rxs, sz, szs, rz, rzs, owned, att, hs, hr,
+    in_sem, out_sem, sp_sem, rp_sem, sx_sem, rx_sem, sz_sem, rz_sem,
+    gzs_sem, gzr_sem, gxs_sem, gxr_sem, hs_sem, hr_sem, as_sem, ar_sem, near_sem, pair_sem,
 ):
     c = lax.axis_index("ctx")
     h = lax.axis_index("head")
@@ -45,6 +45,11 @@
     x, core = g // 2, g % 2
     zh, y = h // 4, h % 4
     zo = OWNER_Z + core
+    owner = zo * 8 + x * 2 + 1
+    partner = z * 8 + x * 2 + (core + 1) % 2
+    owns_even = (core == 1) & (z == OWNER_Z)
+    owns_odd = (core == 1) & (z == OWNER_Z + 1)
+    owned_head = x * 2 + (z + OWNER_Z) % 2
 
     def at_ctx(cc):
         return {"ctx": cc, "head": h}
@@ -129,6 +134,8 @@
         )
 
     others = pl.ds(1, 7)
+    six = pl.ds(1, 6)
+    senders = (1, 2, 3, 4, 6, 7)
 
     def piece(i):
         return slice(i * PIECE, (i + 1) * PIECE)
@@ -150,19 +157,43 @@
         for slot in slots:
             x_copy(i, slot, x_peer(slot // 2, slot % 2)).start()
 
-    option_heads((4, 5, 2, 3))
+    def pair_copy(i):
+        src, dst = (sxs, pxs) if i == PIECES else (sx.at[i], px.at[i])
+        return pltpu.make_async_remote_copy(
+            src_ref=src.at[5], dst_ref=dst, send_sem=sp_sem.at[i], recv_sem=rp_sem.at[i],
+            device_id=at_ctx(partner), device_id_type=MESH,
+        )
+
+    option_heads((5, 4))
     pl.semaphore_wait(barrier, 12)
-    send_heads(PIECES, (4, 5, 2, 3))
-    send_heads(0, (4, 5, 2, 3))
+    for i in (PIECES, *range(PIECES)):
+        pair_copy(i).start()
     for k in (1, 15):
         tell(near_sem.at[0], along_z(k))
 
     arrived(oq_v.at[:, 0 : 4 * HEAD], in_sem.at[1])
-    option_heads((6, 7, 1, 0))
-    send_heads(PIECES, (6, 7, 1))
-    send_heads(0, (6, 7, 1))
+    option_heads((2, 3, 6, 7))
+    send_heads(PIECES, (2, 3, 6, 7))
+    send_heads(0, (2, 3, 6, 7))
+
+    arrived(pxs, rp_sem.at[PIECES])
+    m_here, m_there = sxs[4, 0:1, :], pxs[0:1, :]
+    m_pair = jnp.maximum(m_here, m_there)
+    f_here, f_there = jnp.exp(m_here - m_pair), jnp.exp(m_there - m_pair)
+    l_pair = f_here * sxs[4, 1:2, :] + f_there * pxs[1:2, :]
+    sxs[4, 0:1, :] = m_pair
+    sxs[4, 1:2, :] = l_pair
+    for i in range(PIECES):
+        arrived(px.at[i], rp_sem.at[i])
+        sx[i, 4] = (f_here * sx[i, 4].astype(F32) + f_there * px[i].astype(F32)).astype(BF16)
+    send_heads(PIECES, (4,))
+    for i in range(PIECES):
+        send_heads(i, (4,))
+    option_heads((1, 0))
+    send_heads(PIECES, (1,))
+    send_heads(0, (1,))
     for i in range(1, PIECES):
-        send_heads(i, (4, 5, 2, 3, 6, 7, 1))
+        send_heads(i, (2, 3, 6, 7, 1))
 
     @pl.when(c == 0)
     def _():
@@ -181,7 +212,7 @@
     key_at = lax.broadcasted_iota(jnp.int32, (ROWS, ROWS), 0)
     row_at = lax.broadcasted_iota(jnp.int32, (ROWS, ROWS), 1)
     visible = (seg_row == seg_col) & (row_at >= key_at)
-    q_own = oq_v[:, pl.ds(pl.multiple_of(g * HEAD, HEAD), HEAD)]
+    q_own = oq_v[:, pl.ds(pl.multiple_of(owned_head * HEAD, HEAD), HEAD)]
     vt_self = ov_v[...].astype(F32).T.astype(BF16)
     self_part = partial(q_own, ok_v[...], vt_self, visible)
 
@@ -194,6 +225,10 @@
     for k in (4, 12):
         tell(near_sem.at[2], along_z(k))
 
+    @pl.when(core == 1)
+    def _():
+        tell(pair_sem, at_ctx(partner))
+
     def factors_of(tops):
         top = functools.reduce(jnp.maximum, tops)
         return top, [jnp.exp(m - top) for m in tops]
@@ -205,32 +240,41 @@
             device_id=at_ctx(target), device_id_type=MESH,
         )
 
-    to_owner = (z - zo + NZ) % NZ
-    owner = zo * 8 + g
-    arrived(rxs.at[others], rx_sem.at[PIECES])
-    top, factors = factors_of([sxs[0, 0:1, :]] + [rxs[k, 0:1, :] for k in range(1, 8)])
+    arrived(rxs.at[six], rx_sem.at[PIECES])
+    top, factors = factors_of([sxs[0, 0:1, :]] + [rxs[k, 0:1, :] for k in senders])
     total = factors[0] * sxs[0, 1:2, :]
-    for k in range(1, 8):
-        total = total + factors[k] * rxs[k, 1:2, :]
-
-    @pl.when(z != zo)
+    for n, k in enumerate(senders):
+        total = total + factors[n + 1] * rxs[k, 1:2, :]
+
+    @pl.when(core == 0)
+    def _():
+        pl.semaphore_wait(pair_sem, 1)
+
+    @pl.when(~owns_odd)
     def _():
         szs[0:1, :] = top
         szs[1:2, :] = total
-        z_copy(PIECES, to_owner, owner).start()
-
-    mixes = []
-    for i in range(PIECES):
-        arrived(rx.at[i, others], rx_sem.at[i])
+        z_copy(PIECES, z, owner).start()
+
+    @pl.when(owns_odd)
+    def _():
+        rzs[OWNER_Z + 1, 0:1, :] = top
+        rzs[OWNER_Z + 1, 1:2, :] = total
+
+    for i in range(PIECES):
+        arrived(rx.at[i, six], rx_sem.at[i])
         mix = factors[0] * sx[i, 0].astype(F32)
-        for k in range(1, 8):
-            mix = mix + factors[k] * rx[i, k].astype(F32)
-        mixes.append(mix)
-
-        @pl.when(z != zo)
+        for n, k in enumerate(senders):
+            mix = mix + factors[n + 1] * rx[i, k].astype(F32)
+
+        @pl.when(~owns_odd)
         def _():
             sz[i] = mix.astype(BF16)
-            z_copy(i, to_owner, owner).start()
+            z_copy(i, z, owner).start()
+
+        @pl.when(owns_odd)
+        def _():
+            rz[i, OWNER_Z + 1] = mix.astype(BF16)
 
     at_foot = (z == 0) & (core == 0)
 
@@ -252,7 +296,7 @@
 
     def gz_copy(i, target):
         return pltpu.make_async_remote_copy(
-            src_ref=att.at[i, g], dst_ref=att.at[i, g], send_sem=gzs_sem.at[i], recv_sem=gzr_sem.at[i],
+            src_ref=owned.at[i], dst_ref=att.at[i, owned_head], send_sem=gzs_sem.at[i], recv_sem=gzr_sem.at[i],
             device_id=at_ctx(target), device_id_type=MESH,
         )
 
@@ -266,26 +310,47 @@
         for slot in (4, 5, 2, 3, 6, 7, 1):
             gx_copy(i, x_peer(slot // 2, slot % 2)).start()
 
-    @pl.when(z == zo)
+    def column_arrived(ref, sem):
+        @pl.when(owns_even)
+        def _():
+            arrived(ref, sem)
+
+        @pl.when(owns_odd)
+        def _():
+            arrived(ref.at[others], sem)
+
+    @pl.when(owns_even | owns_odd)
     def _():
         self_top, self_total, self_mix = self_part
-        arrived(rzs.at[others], rz_sem.at[PIECES])
-        _, parts = factors_of([top, self_top] + [rzs[k, 0:1, :] for k in range(1, NZ)])
-        whole = parts[0] * total + parts[1] * self_total
-        for k in range(1, NZ):
+        column_arrived(rzs, rz_sem.at[PIECES])
+        _, parts = factors_of([self_top] + [rzs[k, 0:1, :] for k in range(NZ)])
+        whole = parts[0] * self_total
+        for k in range(NZ):
             whole = whole + parts[k + 1] * rzs[k, 1:2, :]
         for i in range(PIECES):
-            arrived(rz.at[i, others], rz_sem.at[i])
-            summed = parts[0] * mixes[i] + parts[1] * self_mix[piece(i)]
-            for k in range(1, NZ):
+            column_arrived(rz.at[i], rz_sem.at[i])
+            summed = parts[0] * self_mix[piece(i)]
+            for k in range(NZ):
                 summed = summed + parts[k + 1] * rz[i, k].astype(F32)
-            att[i, g] = (summed / whole).astype(BF16)
-            for k in (5, 4, 6, 7, 1, 2, 3):
-                gz_copy(i, ((z + k) % NZ) * 8 + g).start()
+            owned[i] = (summed / whole).astype(BF16)
+
+            @pl.when(owns_odd)
+            def _():
+                att[i, g] = owned[i]
+
+            for k in (0, 1, 2, 7, 3, 6, 5):
+                gz_copy(i, k * 8 + owned_head).start()
+
+            @pl.when(owns_even)
+            def _():
+                gz_copy(i, 4 * 8 + owned_head).start()
+
+    @pl.when(owns_odd)
+    def _():
         for i in range(PIECES):
             gx_send(i)
 
-    @pl.when(z != zo)
+    @pl.when(~owns_odd)
     def _():
         for i in range(PIECES):
             arrived(att.at[i, 0], gzr_sem.at[i])
@@ -366,21 +431,28 @@
             pltpu.make_async_copy(co_v.at[:, cols], ctx_out.at[:, cols], out_sem).start()
 
     arrived(co_v, out_sem)
-    arrived(sxs.at[others], sx_sem.at[PIECES])
+    arrived(sxs.at[six], sx_sem.at[PIECES])
+    arrived(pxs, sp_sem.at[PIECES])
     arrived(hs.at[others], hs_sem)
     for i in range(PIECES):
-        arrived(sx.at[i, others], sx_sem.at[i])
+        arrived(sx.at[i, six], sx_sem.at[i])
+        arrived(px.at[i], sp_sem.at[i])
         arrived(att.at[i, others], gxs_sem.at[i])
 
-    @pl.when(z != zo)
+    @pl.when(~owns_odd)
     def _():
         arrived(szs, sz_sem.at[PIECES])
         for i in range(PIECES):
             arrived(sz.at[i], sz_sem.at[i])
 
-    @pl.when(z == zo)
-    def _():
-        for i in range(PIECES):
+    for i in range(PIECES):
+
+        @pl.when(owns_even)
+        def _():
+            arrived(att.at[i], gzs_sem.at[i])
+
+        @pl.when(owns_odd)
+        def _():
             arrived(att.at[i, others], gzs_sem.at[i])
 
     @pl.when(c == 0)
@@ -442,17 +514,22 @@
             vmem((PIECES, HEAD, GROUPS * PIECE), BF16),
             vmem((PIECES, 8, PIECE, ROWS), BF16),
             vmem((8, 2, ROWS), F32),
+            vmem((PIECES, PIECE, ROWS), BF16),
+            vmem((2, ROWS), F32),
             vmem((PIECES, 8, PIECE, ROWS), BF16),
             vmem((8, 2, ROWS), F32),
             vmem((PIECES, PIECE, ROWS), BF16),
             vmem((2, ROWS), F32),
             vmem((PIECES, 8, PIECE, ROWS), BF16),
             vmem((8, 2, ROWS), F32),
+            vmem((PIECES, PIECE, ROWS), BF16),
             vmem((PIECES, 8, PIECE, ROWS), BF16),
             vmem((8, 16, HEAD), BF16),
             vmem((8, 16, HEAD), BF16),
             dma((7,)),
             dma(()),
+            dma((PIECES + 1,)),
+            dma((PIECES + 1,)),
             dma((PIECES + 1,)),
             dma((PIECES + 1,)),
             dma((PIECES + 1,)),
@@ -466,6 +543,7 @@
             dma((4,)),
             dma((4,)),
             pltpu.SemaphoreType.REGULAR((4,)),
+            pltpu.SemaphoreType.REGULAR,
         ],
         compiler_params=pltpu.CompilerParams(collective_id=0, has_side_effects=True),
     )(cq, ck, cv, oq, ok, ov, seg.reshape(1, ROWS), w)

time: 42.3 us -> 41.9 us (level)
  no operation moved by 1% of the time
where the time goes in v4:
time: 41.9 us; the launch traced here: 41.8 us
  Pallas kernels  41.1 us (98%)
  between operations  0.64 us (2%)
    pallas_call x1, Pallas kernels, layer(): pl.pallas_call(kernel, name='star_attention', out_shape=(vmem((BLOCK, GRO...  40.3 us
    pallas_call x1, Pallas kernels, layer(): pl.pallas_call(put_out, name='put_out', out_shape=(jax.ShapeDtypeStruct((...  0.86 us

profile of v4, /device:TPU:1, one launch (start us, length us, event | category | flops | bytes accessed | tf_op | source)
XLA Modules:
  0.0 41.8 jit_solution(5467964129602398143)
XLA Ops:
  0.6 40.3 %star_attention.1 = (bf16[256,1024]{1,0:T(8,128)(2,1)S(1)}, bf16[16,128]{1,0:T(8,128)(2,1)S(1)}) custom-call(bf16[256,1024]{1,0:T(8,128)(2,1)} %cq.1, bf16[256,128]{1,0:T(8,128)(2,1)} %ck.1, bf16[256,128]{1,0:T(8,128)(2,1)} %cv.1, bf16[128,1024]{1,0:T(8,128)(2,1)} %oq.1, bf16[128,128]{1,0:T(8,128)(2,1)} %ok.1, bf16[128,128]{1,0:T(8,128)(2,1)} %ov.1, ...), custom_call_target="tpu_custom_call" | custom-call | tf_op jit(solution)/shard_map/star_attention/pallas_call | solution.py:499
  40.9 0.9 %put_out.1 = (bf16[256,1024]{1,0:T(8,128)(2,1)}, bf16[16,128]{1,0:T(8,128)(2,1)}) custom-call(bf16[256,1024]{1,0:T(8,128)(2,1)S(1)} %get-tuple-element.4.co, bf16[16,128]{1,0:T(8,128)(2,1)S(1)} %get-tuple-element.5.oo), custom_call_target="tpu_custom_call" | custom-call | tf_op jit(solution)/shard_map/put_out/pallas_call | solution.py:550

commit v5 on v4

--- a/solution.py
+++ b/solution.py
@@ -14,7 +14,7 @@
 GROUPS = 8
 NZ = 8
 OWNER_Z = 3
-PIECES = 2
+PIECES = 4
 PIECE = HEAD // PIECES
 QUARTER = BLOCK // 4
 SCALE = HEAD ** (-0.5)
@@ -74,15 +74,11 @@
 
     def query_load(dx):
         cols = pl.ds(pl.multiple_of(((x + dx) % 4) * 2 * HEAD, 2 * HEAD), 2 * HEAD)
-        return pltpu.make_async_copy(oq.at[:, cols], oq_v.at[:, cols], in_sem.at[0 if dx in (1, 2) else 1])
+        return pltpu.make_async_copy(oq.at[:, cols], oq_v.at[:, cols], in_sem.at[0 if dx == 2 else 1])
 
     pltpu.make_async_copy(ck, kv.at[0, own], in_sem.at[0]).start()
-    for dx in (2, 1):
-        query_load(dx).start()
+    query_load(2).start()
     pltpu.make_async_copy(cv, kv.at[1, own], in_sem.at[0]).start()
-    for dx in (3, 0):
-        query_load(dx).start()
-
     barrier = pltpu.get_barrier_semaphore()
     for slot in range(1, 8):
         tell(barrier, at_ctx(x_peer(slot // 2, slot % 2)))
@@ -90,6 +86,8 @@
         tell(barrier, along_z(k))
     for k in range(1, 4):
         tell(barrier, {"ctx": c, "head": head_peer(0, k)})
+    for dx in (1, 3, 0):
+        query_load(dx).start()
     pltpu.make_async_copy(ok, ok_v, in_sem.at[2]).start()
     pltpu.make_async_copy(ov, ov_v, in_sem.at[2]).start()
     pltpu.make_async_copy(seg, seg_v, in_sem.at[3]).start()
@@ -111,7 +109,7 @@
     def anchor_sent(n, quarters):
         arrived(kv.at[:, 0 : quarters * QUARTER], as_sem.at[n])
 
-    arrived(oq_v, in_sem.at[0])
+    arrived(oq_v.at[:, 0 : 6 * HEAD], in_sem.at[0])
     k_own = kv[0, own, :]
     vt_own = kv[1, own, :].astype(F32).T.astype(BF16)
 
@@ -171,7 +169,7 @@
     for k in (1, 15):
         tell(near_sem.at[0], along_z(k))
 
-    arrived(oq_v.at[:, 0 : 4 * HEAD], in_sem.at[1])
+    arrived(oq_v.at[:, 0 : 6 * HEAD], in_sem.at[1])
     option_heads((2, 3, 6, 7))
     send_heads(PIECES, (2, 3, 6, 7))
     send_heads(0, (2, 3, 6, 7))
@@ -483,10 +481,7 @@
 
 
 def put_out(co, oo, ctx_out, opt_out, sem):
-    copies = [pltpu.make_async_copy(oo, opt_out, sem.at[8])]
-    for n in range(8):
-        rows = pl.ds(n * 32, 32)
-        copies.append(pltpu.make_async_copy(co.at[rows], ctx_out.at[rows], sem.at[n]))
+    copies = [pltpu.make_async_copy(oo, opt_out, sem.at[0]), pltpu.make_async_copy(co, ctx_out, sem.at[1])]
     for copy in copies:
         copy.start()
     for copy in copies:
@@ -556,7 +551,7 @@
         ),
         in_specs=[pl.BlockSpec(memory_space=vmem)] * 2,
         out_specs=(anywhere, anywhere),
-        scratch_shapes=[dma((9,))],
+        scratch_shapes=[dma((2,))],
     )(*[pltpu.with_memory_space_constraint(part, vmem) for part in parts])
 
 

time: 41.9 us -> 41.3 us (0.986)
  Pallas kernels: 41.1 us -> 40.5 us
    pallas_call x1, Pallas kernels: 40.3 us -> 39.7 us  [layer(): pl.pallas_call(kernel, name='star_attention', out_shape=(vmem((BLOCK, GRO...]
where the time goes in v5:
time: 41.3 us; the launch traced here: 41.2 us
  Pallas kernels  40.5 us (98%)
  between operations  0.64 us (2%)
    pallas_call x1, Pallas kernels, layer(): pl.pallas_call(kernel, name='star_attention', out_shape=(vmem((BLOCK, GRO...  39.7 us

profile of v5, /device:TPU:1, one launch (start us, length us, event | category | flops | bytes accessed | tf_op | source)
XLA Modules:
  0.0 41.2 jit_solution(10358730113773559468)
XLA Ops:
  0.6 39.7 %star_attention.1 = (bf16[256,1024]{1,0:T(8,128)(2,1)S(1)}, bf16[16,128]{1,0:T(8,128)(2,1)S(1)}) custom-call(bf16[256,1024]{1,0:T(8,128)(2,1)} %cq.1, bf16[256,128]{1,0:T(8,128)(2,1)} %ck.1, bf16[256,128]{1,0:T(8,128)(2,1)} %cv.1, bf16[128,1024]{1,0:T(8,128)(2,1)} %oq.1, bf16[128,128]{1,0:T(8,128)(2,1)} %ok.1, bf16[128,128]{1,0:T(8,128)(2,1)} %ov.1, ...), custom_call_target="tpu_custom_call" | custom-call | tf_op jit(solution)/shard_map/star_attention/pallas_call | solution.py:494
  40.3 0.8 %put_out.1 = (bf16[256,1024]{1,0:T(8,128)(2,1)}, bf16[16,128]{1,0:T(8,128)(2,1)}) custom-call(bf16[256,1024]{1,0:T(8,128)(2,1)S(1)} %get-tuple-element.4.co, bf16[16,128]{1,0:T(8,128)(2,1)S(1)} %get-tuple-element.5.oo), custom_call_target="tpu_custom_call" | custom-call | tf_op jit(solution)/shard_map/put_out/pallas_call | solution.py:545

commit v6 on v5

--- a/solution.py
+++ b/solution.py
@@ -127,7 +127,7 @@
         src, dst = (sxs, rxs) if i == PIECES else (sx.at[i], rx.at[i])
         return pltpu.make_async_remote_copy(
             src_ref=src.at[slot], dst_ref=dst.at[slot],
-            send_sem=sx_sem.at[i], recv_sem=rx_sem.at[i],
+            send_sem=sx_sem.at[i // PIECES], recv_sem=rx_sem.at[i],
             device_id=at_ctx(target), device_id_type=MESH,
         )
 
@@ -158,7 +158,7 @@
     def pair_copy(i):
         src, dst = (sxs, pxs) if i == PIECES else (sx.at[i], px.at[i])
         return pltpu.make_async_remote_copy(
-            src_ref=src.at[5], dst_ref=dst, send_sem=sp_sem.at[i], recv_sem=rp_sem.at[i],
+            src_ref=src.at[5], dst_ref=dst, send_sem=sp_sem.at[i // PIECES], recv_sem=rp_sem.at[i // PIECES],
             device_id=at_ctx(partner), device_id_type=MESH,
         )
 
@@ -174,24 +174,23 @@
     send_heads(PIECES, (2, 3, 6, 7))
     send_heads(0, (2, 3, 6, 7))
 
-    arrived(pxs, rp_sem.at[PIECES])
+    arrived(pxs, rp_sem.at[1])
     m_here, m_there = sxs[4, 0:1, :], pxs[0:1, :]
     m_pair = jnp.maximum(m_here, m_there)
     f_here, f_there = jnp.exp(m_here - m_pair), jnp.exp(m_there - m_pair)
     l_pair = f_here * sxs[4, 1:2, :] + f_there * pxs[1:2, :]
     sxs[4, 0:1, :] = m_pair
     sxs[4, 1:2, :] = l_pair
+    arrived(px, rp_sem.at[0])
     for i in range(PIECES):
-        arrived(px.at[i], rp_sem.at[i])
         sx[i, 4] = (f_here * sx[i, 4].astype(F32) + f_there * px[i].astype(F32)).astype(BF16)
     send_heads(PIECES, (4,))
-    for i in range(PIECES):
-        send_heads(i, (4,))
+    send_heads(0, (4,))
     option_heads((1, 0))
     send_heads(PIECES, (1,))
     send_heads(0, (1,))
     for i in range(1, PIECES):
-        send_heads(i, (2, 3, 6, 7, 1))
+        send_heads(i, (4, 2, 3, 6, 7, 1))
 
     @pl.when(c == 0)
     def _():
@@ -234,7 +233,7 @@
     def z_copy(i, k, target):
         src, dst = (szs, rzs) if i == PIECES else (sz.at[i], rz.at[i])
         return pltpu.make_async_remote_copy(
-            src_ref=src, dst_ref=dst.at[k], send_sem=sz_sem.at[i], recv_sem=rz_sem.at[i],
+            src_ref=src, dst_ref=dst.at[k], send_sem=sz_sem.at[i // PIECES], recv_sem=rz_sem.at[i],
             device_id=at_ctx(target), device_id_type=MESH,
         )
 
@@ -294,13 +293,13 @@
 
     def gz_copy(i, target):
         return pltpu.make_async_remote_copy(
-            src_ref=owned.at[i], dst_ref=att.at[i, owned_head], send_sem=gzs_sem.at[i], recv_sem=gzr_sem.at[i],
+            src_ref=owned.at[i], dst_ref=att.at[i, owned_head], send_sem=gzs_sem, recv_sem=gzr_sem.at[i],
             device_id=at_ctx(target), device_id_type=MESH,
         )
 
     def gx_copy(i, target):
         return pltpu.make_async_remote_copy(
-            src_ref=att.at[i, g], dst_ref=att.at[i, g], send_sem=gxs_sem.at[i], recv_sem=gxr_sem.at[i],
+            src_ref=att.at[i, g], dst_ref=att.at[i, g], send_sem=gxs_sem, recv_sem=gxr_sem.at[i],
             device_id=at_ctx(target), device_id_type=MESH,
         )
 
@@ -429,29 +428,25 @@
             pltpu.make_async_copy(co_v.at[:, cols], ctx_out.at[:, cols], out_sem).start()
 
     arrived(co_v, out_sem)
-    arrived(sxs.at[six], sx_sem.at[PIECES])
-    arrived(pxs, sp_sem.at[PIECES])
+    arrived(sxs.at[six], sx_sem.at[1])
+    arrived(pxs, sp_sem.at[1])
     arrived(hs.at[others], hs_sem)
-    for i in range(PIECES):
-        arrived(sx.at[i, six], sx_sem.at[i])
-        arrived(px.at[i], sp_sem.at[i])
-        arrived(att.at[i, others], gxs_sem.at[i])
+    arrived(sx.at[:, six], sx_sem.at[0])
+    arrived(px, sp_sem.at[0])
+    arrived(att.at[:, others], gxs_sem)
 
     @pl.when(~owns_odd)
     def _():
-        arrived(szs, sz_sem.at[PIECES])
-        for i in range(PIECES):
-            arrived(sz.at[i], sz_sem.at[i])
-
-    for i in range(PIECES):
-
-        @pl.when(owns_even)
-        def _():
-            arrived(att.at[i], gzs_sem.at[i])
-
-        @pl.when(owns_odd)
-        def _():
-            arrived(att.at[i, others], gzs_sem.at[i])
+        arrived(szs, sz_sem.at[1])
+        arrived(sz, sz_sem.at[0])
+
+    @pl.when(owns_even)
+    def _():
+        arrived(att, gzs_sem)
+
+    @pl.when(owns_odd)
+    def _():
+        arrived(att.at[:, others], gzs_sem)
 
     @pl.when(c == 0)
     def _():
@@ -523,15 +518,15 @@
             vmem((8, 16, HEAD), BF16),
             dma((7,)),
             dma(()),
+            dma((2,)),
+            dma((2,)),
+            dma((2,)),
             dma((PIECES + 1,)),
+            dma((2,)),
             dma((PIECES + 1,)),
-            dma((PIECES + 1,)),
-            dma((PIECES + 1,)),
-            dma((PIECES + 1,)),
-            dma((PIECES + 1,)),
+            dma(()),
             dma((PIECES,)),
-            dma((PIECES,)),
-            dma((PIECES,)),
+            dma(()),
             dma((PIECES,)),
             dma(()),
             dma(()),

time: 41.3 us -> 41 us (level)
  no operation moved by 1% of the time
where the time goes in v6:
time: 41 us; the launch traced here: 40.8 us
  Pallas kernels  40.2 us (98%)
  between operations  0.64 us (2%)
    pallas_call x1, Pallas kernels, layer(): pl.pallas_call(kernel, name='star_attention', out_shape=(vmem((BLOCK, GRO...  39.4 us

profile of v6, /device:TPU:1, one launch (start us, length us, event | category | flops | bytes accessed | tf_op | source)
XLA Modules:
  0.0 40.8 jit_solution(16849565936579549290)
XLA Ops:
  0.6 39.4 %star_attention.1 = (bf16[256,1024]{1,0:T(8,128)(2,1)S(1)}, bf16[16,128]{1,0:T(8,128)(2,1)S(1)}) custom-call(bf16[256,1024]{1,0:T(8,128)(2,1)} %cq.1, bf16[256,128]{1,0:T(8,128)(2,1)} %ck.1, bf16[256,128]{1,0:T(8,128)(2,1)} %cv.1, bf16[128,1024]{1,0:T(8,128)(2,1)} %oq.1, bf16[128,128]{1,0:T(8,128)(2,1)} %ok.1, bf16[128,128]{1,0:T(8,128)(2,1)} %ov.1, ...), custom_call_target="tpu_custom_call" | custom-call | tf_op jit(solution)/shard_map/star_attention/pallas_call | solution.py:489
  40.0 0.8 %put_out.1 = (bf16[256,1024]{1,0:T(8,128)(2,1)}, bf16[16,128]{1,0:T(8,128)(2,1)}) custom-call(bf16[256,1024]{1,0:T(8,128)(2,1)S(1)} %get-tuple-element.4.co, bf16[16,128]{1,0:T(8,128)(2,1)S(1)} %get-tuple-element.5.oo), custom_call_target="tpu_custom_call" | custom-call | tf_op jit(solution)/shard_map/put_out/pallas_call | solution.py:540

commit v7 on v6

--- a/solution.py
+++ b/solution.py
@@ -174,6 +174,10 @@
     send_heads(PIECES, (2, 3, 6, 7))
     send_heads(0, (2, 3, 6, 7))
 
+    option_heads((1, 0))
+    send_heads(PIECES, (1,))
+    send_heads(0, (1,))
+
     arrived(pxs, rp_sem.at[1])
     m_here, m_there = sxs[4, 0:1, :], pxs[0:1, :]
     m_pair = jnp.maximum(m_here, m_there)
@@ -186,9 +190,6 @@
         sx[i, 4] = (f_here * sx[i, 4].astype(F32) + f_there * px[i].astype(F32)).astype(BF16)
     send_heads(PIECES, (4,))
     send_heads(0, (4,))
-    option_heads((1, 0))
-    send_heads(PIECES, (1,))
-    send_heads(0, (1,))
     for i in range(1, PIECES):
         send_heads(i, (4, 2, 3, 6, 7, 1))
 

time: 41 us -> 41.3 us (level)
  no operation moved by 1% of the time
where the time goes in v7:
time: 41.3 us; the launch traced here: 41.2 us
  Pallas kernels  40.5 us (98%)
  between operations  0.64 us (2%)
    pallas_call x1, Pallas kernels, layer(): pl.pallas_call(kernel, name='star_attention', out_shape=(vmem((BLOCK, GRO...  39.7 us

profile of v7, /device:TPU:1, one launch (start us, length us, event | category | flops | bytes accessed | tf_op | source)
XLA Modules:
  0.0 41.2 jit_solution(948556314859931354)
XLA Ops:
  0.6 39.7 %star_attention.1 = (bf16[256,1024]{1,0:T(8,128)(2,1)S(1)}, bf16[16,128]{1,0:T(8,128)(2,1)S(1)}) custom-call(bf16[256,1024]{1,0:T(8,128)(2,1)} %cq.1, bf16[256,128]{1,0:T(8,128)(2,1)} %ck.1, bf16[256,128]{1,0:T(8,128)(2,1)} %cv.1, bf16[128,1024]{1,0:T(8,128)(2,1)} %oq.1, bf16[128,128]{1,0:T(8,128)(2,1)} %ok.1, bf16[128,128]{1,0:T(8,128)(2,1)} %ov.1, ...), custom_call_target="tpu_custom_call" | custom-call | tf_op jit(solution)/shard_map/star_attention/pallas_call | solution.py:490
  40.4 0.8 %put_out.1 = (bf16[256,1024]{1,0:T(8,128)(2,1)}, bf16[16,128]{1,0:T(8,128)(2,1)}) custom-call(bf16[256,1024]{1,0:T(8,128)(2,1)S(1)} %get-tuple-element.4.co, bf16[16,128]{1,0:T(8,128)(2,1)S(1)} %get-tuple-element.5.oo), custom_call_target="tpu_custom_call" | custom-call | tf_op jit(solution)/shard_map/put_out/pallas_call | solution.py:541
